TPU v7x, 512 devices: a whole 4x8x8 slice. The times are simulated.
512 devices in a mesh: rows: 32 (over z, x), cols: 16 (over y, core).
Axes of the slice: x: 4, y: 8, z: 8, core: 2. Of those that a mesh axis runs over, the one named last changes fastest.
Arguments:
- tokens: bfloat16 [8192, 4096], P('rows', 'cols'), may hold values from -6 to 6
- cotangent: bfloat16 [8192, 4096], P('rows', 'cols'), may hold values from -6 to 6
- gate_weight: bfloat16 [4096, 7168], P('rows', 'cols'), may hold values from -0.09375 to 0.09375
- down_weight: bfloat16 [4096, 7168], P('rows', 'cols'), may hold values from -0.0625 to 0.0625
- proj_in: bfloat16 [4096, 128], replicated, may hold values from -0.09375 to 0.09375
- proj_out: bfloat16 [7168, 64], P('cols'), may hold values from -0.0625 to 0.0625
- lengths: int32 [128], P('rows'), may hold values from 16 to 64
- loss_mask: int32 [128, 64], P('rows'), may hold values 0 or 1
- gram_in: float32 [8, 1024, 8, 1024], P(None, 'rows', None, 'cols'), as said below
- queries: float32 [256, 8, 1024], P('cols', None, 'rows'), may hold values from -6 to 6
Outputs:
- gram_next: float32 [8, 1024, 8, 1024], P(None, 'rows', None, 'cols')
- query_next: float32 [256, 8, 1024], P('cols', None, 'rows')
- scores: float32 [256, 128], P('cols', 'rows')
Inputs may be any that keep to these rules, and one draw needn't show every extreme that they name: gram_in, read as a 8192 x 8192 matrix, is symmetric positive definite.
All inputs are finite; a program needn't handle non-finite values. No bound on the sum of `loss_mask` on one device may be relied on, other than what follows from the above.
Results may differ from a plain program's by a relative error of at most 0.004.
Values may be sent and summed in bfloat16 or wider, within the bound.
A program may use at most 128 MiB of HBM per device.

v0:
```python
import jax
import jax.numpy as jnp
from jax import lax
from jax.sharding import Mesh
from jax.sharding import PartitionSpec as P

COLS = ("cols_0", "cols_1")


highest = lax.Precision.HIGHEST


def sent_together(arrays, axis, dim, along):
    widths = [a.shape[along] for a in arrays]
    both = jnp.concatenate(arrays, axis=along)
    filled = lax.all_gather(both, axis, axis=dim, tiled=True)
    return tuple(jnp.split(filled, [sum(widths[:k]) for k in range(1, len(widths))], axis=along))


def over_pieces(x, axis):
    tiles = lax.all_gather(x, axis)
    return tiles.sum(axis=0)


def joined_along(tiles, dim):
    lengths = list(tiles.shape[1:])
    lengths[dim] *= tiles.shape[0]
    return jnp.moveaxis(tiles, 0, dim).reshape(lengths)


def copy_for_each(x, axis):
    size = lax.axis_size(axis)
    return lax.all_to_all(jnp.broadcast_to(x[None], (size, *x.shape)), axis, 0, 0, tiled=True)


def gathered_copies(x, axis, dim):
    return joined_along(copy_for_each(x, axis), dim)


def gathered_by_axis(x, axes, dim):
    for axis in reversed(axes):
        x = lax.all_gather(x, axis, axis=dim, tiled=True)
    return x


def local(
    tokens,
    cotangent,
    gate_weight,
    down_weight,
    proj_in,
    proj_out,
    lengths,
    loss_mask,
    gram_in,
    queries,
):
    row_count = lax.axis_size("rows")
    row_index = lax.axis_index("rows")
    col_index = lax.axis_index(COLS)
    full_tokens, full_cotangent = sent_together((tokens, cotangent), COLS, 1, 0)
    pieces = sent_together((gate_weight, down_weight), "rows", 0, 1)
    gate_pre = jnp.dot(full_tokens, pieces[0], preferred_element_type=jnp.float32)
    grad_hidden = jnp.dot(full_cotangent, pieces[1], preferred_element_type=jnp.float32)
    grad_up = (grad_hidden * jax.nn.silu(gate_pre)).astype(jnp.bfloat16)
    outer_part = jnp.dot(grad_up, proj_out, preferred_element_type=jnp.float32)
    proj_inner = jnp.dot(full_tokens, proj_in, preferred_element_type=jnp.float32)
    proj_outer = over_pieces(outer_part, COLS)
    seq_count, window = loss_mask.shape
    inner_width = proj_in.shape[1]
    outer_width = proj_out.shape[1]
    positions = jnp.arange(window, dtype=jnp.int32)
    token_live = (positions[None, :] >= (window - lengths)[:, None]).astype(
        jnp.float32
    ) * loss_mask.astype(jnp.float32)
    weighted = proj_inner.reshape(seq_count, window, inner_width) * token_live[:, :, None]
    features = jnp.einsum(
        "stk,stl->skl",
        weighted,
        proj_outer.reshape(seq_count, window, outer_width),
        precision=highest,
    )
    cycles, band_rows, _, band_cols = gram_in.shape
    panel_width = band_rows * row_count
    features = features.reshape(seq_count, cycles, panel_width)
    by_owner = features.reshape(seq_count, cycles, row_count, band_rows)
    row_part = lax.all_to_all(by_owner, "rows", split_axis=2, concat_axis=0, tiled=True).reshape(
        seq_count * row_count, cycles, band_rows
    )
    own_cols = lax.dynamic_slice_in_dim(features, col_index * band_cols, band_cols, 2)
    col_part = gathered_copies(own_cols, "rows", 0)
    seq_total = row_part.shape[0]
    row_flat = row_part.reshape(seq_total, cycles * band_rows)
    col_flat = col_part.reshape(seq_total, cycles * band_cols)
    update = (
        jnp.dot(row_flat.T, col_flat, precision=highest, preferred_element_type=jnp.float32)
        / seq_total
    )
    updated = gram_in + update.reshape(cycles, band_rows, cycles, band_cols)
    panel_rows = gathered_by_axis(updated[:, :, 0, :], COLS, 2)
    query_heads = jnp.transpose(queries[:, 0, :])
    diag_block, head_cols = sent_together((panel_rows[0], query_heads), "rows", 0, 1)
    factor = jnp.linalg.cholesky(diag_block)
    below_rows = panel_rows[1:].reshape((cycles - 1) * band_rows, panel_width)
    lower_part = jax.scipy.linalg.solve_triangular(factor, below_rows.T, lower=True).T
    own_factor = lax.dynamic_slice_in_dim(factor, row_index * band_rows, band_rows, 0)
    column_block = jnp.concatenate(
        [own_factor[None], lower_part.reshape(cycles - 1, band_rows, panel_width)], axis=0
    )
    panel_part = lax.dynamic_slice_in_dim(column_block, col_index * band_cols, band_cols, 2)
    gram_next = updated.at[:, :, 0, :].set(panel_part)
    query_count = queries.shape[0]
    solved = jax.scipy.linalg.solve_triangular(factor, head_cols, lower=True)
    query_tail = queries[:, 1:, :].reshape(query_count, (cycles - 1) * band_rows) - jnp.dot(
        solved.T, lower_part.T, precision=highest, preferred_element_type=jnp.float32
    )
    own_head = jnp.transpose(lax.dynamic_slice_in_dim(solved, row_index * band_rows, band_rows, 0))
    query_next = jnp.concatenate(
        [own_head[:, None, :], query_tail.reshape(query_count, cycles - 1, band_rows)], axis=1
    )
    whitened = jax.scipy.linalg.solve_triangular(factor, features[:, 0, :].T, lower=True)
    scores = jnp.dot(solved.T, whitened, precision=highest, preferred_element_type=jnp.float32)
    return (gram_next, query_next, scores)


def solution(mesh):
    finer = Mesh(mesh.devices.reshape(mesh.shape["rows"], 8, 2), ("rows", "cols_0", "cols_1"))
    return jax.shard_map(
        local,
        mesh=finer,
        in_specs=(
            P("rows", COLS),
            P("rows", COLS),
            P("rows", COLS),
            P("rows", COLS),
            P(),
            P(COLS, None),
            P("rows"),
            P("rows", None),
            P(None, "rows", None, COLS),
            P(COLS, None, "rows"),
        ),
        out_specs=(P(None, "rows", None, COLS), P(COLS, None, "rows"), P(COLS, "rows")),
        check_vma=False,
    )
```

profile of v0, /device:TPU:1, one launch (start us, length us, event | category | flops | bytes accessed | tf_op | source)
XLA Modules:
  0.0 761.6 jit_solution(9495188101314995122)
XLA Ops:
  7.2 1.8 pad_maximum_fusion
  9.1 1.7 pad_maximum_fusion.1
  10.8 58.2 %all-gather.9.cloned.1.call-done = bf16[512,4096]{1,0:T(8,128)(2,1)} async-done(((bf16[512,256]{1,0:T(8,128)(2,1)}), bf16[512,4096]{1,0:T(8,128)(2,1)}) %all-gather.9.cloned.1.call-update) | async-done | bytes 4194320 | tf_op jit(solution)/shard_map/all_gather | solution.py:16
  69.0 100.6 %all-gather.11.cloned.1.call-done = bf16[4096,896]{0,1:T(8,128)(2,1)} async-done(((bf16[128,896]{0,1:T(8,128)(2,1)}), bf16[4096,896]{0,1:T(8,128)(2,1)}) %all-gather.11.cloned.1.call-update) | async-done | bytes 7340048 | tf_op jit(solution)/shard_map/all_gather | solution.py:16
  169.6 3.8 fusion.2
  173.5 4.7 fusion.22
  178.3 2.3 fusion.8
  180.6 41.6 %all-gather.15.cloned.1.call-done = f32[4096,64]{0,1:T(8,128)} async-done(((f32[256,64]{0,1:T(8,128)}), f32[4096,64]{0,1:T(8,128)}) %all-gather.15.cloned.1.call-update) | async-done | bytes 1048592 | tf_op jit(solution)/shard_map/all_gather | solution.py:21
  222.2 1.5 copy.77
  226.1 9.9 %all-to-all-start = ((f32[32,1,1024]{2,1,0:T(1,128)}), f32[32,1,1024]{2,1,0:T(1,128)S(1)}, u32[]{:S(2)}, u32[]{:S(2)}) async-start(f32[32,1,1024]{2,1,0:T(1,128)} %reshape.234), calls=%async_computation | async-start | bytes 262144 | tf_op jit(solution)/shard_map/all_to_all | solution.py:87
  237.3 8.1 %all-to-all-done = f32[32,1,1024]{2,1,0:T(1,128)S(1)} async-done(((f32[32,1,1024]{2,1,0:T(1,128)}), f32[32,1,1024]{2,1,0:T(1,128)S(1)}, u32[]{:S(2)}, u32[]{:S(2)}) %all-to-all-start) | async-done | bytes 131104 | tf_op jit(solution)/shard_map/all_to_all | solution.py:87
  245.4 3.9 all-to-all-start.1
  251.2 8.5 %all-to-all-done.1 = f32[32,1,2048]{2,1,0:T(1,128)S(1)} async-done(((f32[32,1,2048]{2,1,0:T(1,128)}), f32[32,1,2048]{2,1,0:T(1,128)S(1)}, u32[]{:S(2)}, u32[]{:S(2)}) %all-to-all-start.1) | async-done | bytes 262176 | tf_op jit(solution)/shard_map/all_to_all | solution.py:33
  259.7 1.3 reduce.51
  263.5 5.6 all-gather.1
  270.1 28.8 %all-gather.17.cloned.1.call-done = f32[8,32,1,1024]{3,1,0,2:T(8,128)} async-done(((f32[8,32,1,128]{3,1,0,2:T(8,128)}), f32[8,32,1,1024]{3,1,0,2:T(8,128)}) %all-gather.17.cloned.1.call-update) | async-done | bytes 1048592 | tf_op jit(solution)/shard_map/all_gather | solution.py:42
  300.7 1.2 slice.456
  302.0 90.2 %all-gather.13.cloned.1.call-done = f32[1024,1040]{1,0:T(8,128)} async-done(((f32[32,1040]{1,0:T(8,128)}), f32[1024,1040]{1,0:T(8,128)}) %all-gather.13.cloned.1.call-update) | async-done | bytes 4259856 | tf_op jit(solution)/shard_map/all_gather | solution.py:16
  392.1 4.8 split.25
  397.0 5.5 copy.68
  402.5 4.4 fusion
  406.9 2.0 copy-done.3
  409.0 11.7 %cholesky.223 = f32[128,128]{1,0:T(8,128)S(1)} custom-call(f32[128,128]{1,0:T(8,128)S(1)} %cholesky.580), custom_call_target="Cholesky" | custom-call | tf_op jit(solution)/shard_map/jit(cholesky)/cholesky | solution.py:103
  420.7 9.8 %custom-call.69 = f32[1,128,128]{1,2,0:T(8,128)S(1)} custom-call(f32[1,128,128]{2,1,0:T(8,128)S(1)} %get-tuple-element.94), custom_call_target="InvertDiagBlocksLowerTriangular" | custom-call | tf_op jit(solution)/shard_map/jit(cholesky)/cholesky | solution.py:103
  430.6 2.5 cholesky.255
  433.0 2.4 constant_dynamic-update-slice_fusion.75
  435.4 1.5 convolution_subtract_fusion
  436.9 11.9 %cholesky.244 = f32[128,128]{1,0:T(8,128)S(1)} custom-call(f32[128,128]{1,0:T(8,128)S(1)} %cholesky.584), custom_call_target="Cholesky" | custom-call | tf_op jit(solution)/shard_map/jit(cholesky)/cholesky | solution.py:103
  449.5 9.8 %custom-call.70 = f32[1,128,128]{1,2,0:T(8,128)S(1)} custom-call(f32[1,128,128]{2,1,0:T(8,128)S(1)} %get-tuple-element.91), custom_call_target="InvertDiagBlocksLowerTriangular" | custom-call | tf_op jit(solution)/shard_map/jit(cholesky)/cholesky | solution.py:103
  460.5 2.1 convolution_subtract_fusion.1
  462.7 11.7 %cholesky.468 = f32[128,128]{1,0:T(8,128)S(1)} custom-call(f32[128,128]{1,0:T(8,128)S(1)} %cholesky.589), custom_call_target="Cholesky" | custom-call | tf_op jit(solution)/shard_map/jit(cholesky)/cholesky | solution.py:103
  475.6 9.8 %custom-call.71 = f32[1,128,128]{1,2,0:T(8,128)S(1)} custom-call(f32[1,128,128]{2,1,0:T(8,128)S(1)} %get-tuple-element.88), custom_call_target="InvertDiagBlocksLowerTriangular" | custom-call | tf_op jit(solution)/shard_map/jit(cholesky)/cholesky | solution.py:103
  486.6 2.3 convolution_subtract_fusion.2
  489.0 12.1 %cholesky.487 = f32[128,128]{1,0:T(8,128)S(1)} custom-call(f32[128,128]{1,0:T(8,128)S(1)} %cholesky.594), custom_call_target="Cholesky" | custom-call | tf_op jit(solution)/shard_map/jit(cholesky)/cholesky | solution.py:103
  502.4 9.8 %custom-call.72 = f32[1,128,128]{1,2,0:T(8,128)S(1)} custom-call(f32[1,128,128]{2,1,0:T(8,128)S(1)} %get-tuple-element.85), custom_call_target="InvertDiagBlocksLowerTriangular" | custom-call | tf_op jit(solution)/shard_map/jit(cholesky)/cholesky | solution.py:103
  513.3 2.4 convolution_subtract_fusion.3
  515.7 11.7 %cholesky.506 = f32[128,128]{1,0:T(8,128)S(1)} custom-call(f32[128,128]{1,0:T(8,128)S(1)} %cholesky.599), custom_call_target="Cholesky" | custom-call | tf_op jit(solution)/shard_map/jit(cholesky)/cholesky | solution.py:103
  528.8 9.9 %custom-call.73 = f32[1,128,128]{1,2,0:T(8,128)S(1)} custom-call(f32[1,128,128]{2,1,0:T(8,128)S(1)} %get-tuple-element.82), custom_call_target="InvertDiagBlocksLowerTriangular" | custom-call | tf_op jit(solution)/shard_map/jit(cholesky)/cholesky | solution.py:103
  539.7 2.3 convolution_subtract_fusion.4
  542.0 11.7 %cholesky.526 = f32[128,128]{1,0:T(8,128)S(1)} custom-call(f32[128,128]{1,0:T(8,128)S(1)} %cholesky.604), custom_call_target="Cholesky" | custom-call | tf_op jit(solution)/shard_map/jit(cholesky)/cholesky | solution.py:103
  555.1 9.8 %custom-call.74 = f32[1,128,128]{1,2,0:T(8,128)S(1)} custom-call(f32[1,128,128]{2,1,0:T(8,128)S(1)} %get-tuple-element.79), custom_call_target="InvertDiagBlocksLowerTriangular" | custom-call | tf_op jit(solution)/shard_map/jit(cholesky)/cholesky | solution.py:103
  565.8 2.0 convolution_subtract_fusion.5
  567.9 11.9 %cholesky.546 = f32[128,128]{1,0:T(8,128)S(1)} custom-call(f32[128,128]{1,0:T(8,128)S(1)} %cholesky.609), custom_call_target="Cholesky" | custom-call | tf_op jit(solution)/shard_map/jit(cholesky)/cholesky | solution.py:103
  581.0 9.8 %custom-call.75 = f32[1,128,128]{1,2,0:T(8,128)S(1)} custom-call(f32[1,128,128]{2,1,0:T(8,128)S(1)} %get-tuple-element.76), custom_call_target="InvertDiagBlocksLowerTriangular" | custom-call | tf_op jit(solution)/shard_map/jit(cholesky)/cholesky | solution.py:103
  591.7 1.9 convolution_subtract_fusion.13
  593.6 11.7 %cholesky.564 = f32[128,128]{1,0:T(8,128)S(1)} custom-call(f32[128,128]{1,0:T(8,128)S(1)} %convolution_subtract_fusion.13), custom_call_target="Cholesky" | custom-call | tf_op jit(solution)/shard_map/jit(cholesky)/cholesky | solution.py:103
  612.2 6.7 fusion.1
  618.9 23.2 %while.2 = (s32[]{:T(128)}, f32[1024,1024]{1,0:T(8,128)}, s32[8,2]{0,1:T(2,128)S(1)}, f32[8,128,128]{2,1,0:T(8,128)S(1)}, s32[]{:T(128)}) while((s32[]{:T(128)}, f32[1024,1024]{1,0:T(8,128)}, s32[8,2]{0,1:T(2,128)S(1)}, f32[8,128,128]{2,1,0:T(8,128)S(1)}, s32[]{:T(128)}) %tuple.118), condition=%wide.while_cond.1, body=%wide.while_body.1.sunk | while | flops 2 | bytes 131181 | solution.py:105
  619.4 2.3 bitcast_dynamic-update-slice_fusion.2
  622.4 2.3 bitcast_dynamic-update-slice_fusion.2
  625.3 2.3 bitcast_dynamic-update-slice_fusion.2
  628.2 2.3 bitcast_dynamic-update-slice_fusion.2
  631.1 2.3 bitcast_dynamic-update-slice_fusion.2
  634.0 2.3 bitcast_dynamic-update-slice_fusion.2
  636.9 2.3 bitcast_dynamic-update-slice_fusion.2
  639.8 2.2 bitcast_dynamic-update-slice_fusion.2
  642.1 78.8 %custom-call.76 = f32[8,128,128]{1,2,0:T(8,128)S(1)} custom-call(f32[8,128,128]{2,1,0:T(8,128)S(1)} %get-tuple-element.22), custom_call_target="InvertDiagBlocksLowerTriangular" | custom-call | tf_op jit(solution)/shard_map/jit(_solve_triangular)/triangular_solve | solution.py:105
  726.5 1.4 convolution_subtract_fusion.23
  728.1 1.4 convolution_subtract_fusion.28
  729.7 1.5 convolution_subtract_fusion.22
  733.1 1.3 convolution_subtract_fusion.9
  734.6 1.3 convolution_subtract_fusion.11
  736.1 1.4 convolution_subtract_fusion.12
  749.4 4.6 scatter.4
  (164 shorter events, 51.9 us)
Async XLA Ops:
  7.2 171.1 %copy-start = (bf16[4096,128]{1,0:T(8,128)(2,1)S(1)}, bf16[4096,128]{1,0:T(8,128)(2,1)}, u32[]{:S(2)}) copy-start(bf16[4096,128]{1,0:T(8,128)(2,1)} %param.16) | copy-start | bytes 3145732
  7.2 61.9 %all-gather.9.cloned.1.call-start = ((), (), s32[]{:S(2)}) async-start(), calls=%async_computation.2 | async-start | bytes 4456448 | tf_op jit(solution)/shard_map/all_gather | solution.py:16
  9.0 160.6 %all-gather.11.cloned.1.call-start = ((), (), s32[]{:S(2)}) async-start(), calls=%async_computation.3 | async-start | bytes 7569408 | tf_op jit(solution)/shard_map/all_gather | solution.py:16
  10.8 162.7 %copy-start.8 = (bf16[448,64]{0,1:T(8,128)(2,1)S(1)}, bf16[448,64]{0,1:T(8,128)(2,1)}, u32[]{:S(2)}) copy-start(bf16[448,64]{0,1:T(8,128)(2,1)} %param.17) | copy-start | bytes 172036
  10.8 211.4 %all-gather.15.cloned.1.call-start = ((), (), s32[]{:S(2)}) async-start(), calls=%async_computation.5 | async-start | bytes 1114112 | tf_op jit(solution)/shard_map/all_gather | solution.py:21
  173.4 4.7 copy-start.9
  173.4 4.7 copy-start.7
  226.1 19.4 %all-to-all-start = ((f32[32,1,1024]{2,1,0:T(1,128)}), f32[32,1,1024]{2,1,0:T(1,128)S(1)}, u32[]{:S(2)}, u32[]{:S(2)}) async-start(f32[32,1,1024]{2,1,0:T(1,128)} %reshape.234), calls=%async_computation | async-start | bytes 262144 | tf_op jit(solution)/shard_map/all_to_all | solution.py:87
  236.2 25.9 %copy-start.5 = (f32[8,32,8,64]{3,2,1,0:T(8,128)S(1)}, f32[8,32,8,64]{3,2,1,0:T(8,128)}, u32[]{:S(2)}) copy-start(f32[8,32,8,64]{3,2,1,0:T(8,128)} %param.20) | copy-start | bytes 1572868
  245.4 14.3 %all-to-all-start.1 = ((f32[32,1,2048]{2,1,0:T(1,128)}), f32[32,1,2048]{2,1,0:T(1,128)S(1)}, u32[]{:S(2)}, u32[]{:S(2)}) async-start(f32[32,1,2048]{2,1,0:T(1,128)} %reshape.236), calls=%async_computation.1 | async-start | bytes 524288 | tf_op jit(solution)/shard_map/all_to_all | solution.py:33
  249.3 49.6 %all-gather.17.cloned.1.call-start = ((), (), s32[]{:S(2)}) async-start(), calls=%async_computation.6 | async-start | bytes 1179648 | tf_op jit(solution)/shard_map/all_gather | solution.py:42
  261.2 8.8 %slice-start = ((f32[16,8,32]{2,1,0:T(8,128)}), f32[16,1,32]{2,1,0:T(1,128)S(1)}, s32[]{:S(2)}) async-start(f32[16,8,32]{2,1,0:T(8,128)} %param.21), calls=%async_computation.7 | async-start | bytes 16384 | tf_op jit(solution)/shard_map/slice | solution.py:101
  261.3 39.2 %copy-start.6 = (f32[16,8,32]{2,1,0:T(8,128)S(1)}, f32[16,8,32]{2,1,0:T(8,128)}, u32[]{:S(2)}) copy-start(f32[16,8,32]{2,1,0:T(8,128)} %param.21) | copy-start | bytes 49156
  262.3 1.0 copy-start.4
  270.0 122.2 %all-gather.13.cloned.1.call-start = ((), (), s32[]{:S(2)}) async-start(), calls=%async_computation.4 | async-start | bytes 4866048 | tf_op jit(solution)/shard_map/all_gather | solution.py:16
  406.9 2.0 copy-start.3
  732.8 5.0 copy-start.2
  740.2 14.4 %copy-start.1 = (bf16[4096,128]{1,0:T(8,128)(2,1)S(1)}, bf16[4096,128]{1,0:T(8,128)(2,1)}, u32[]{:S(2)}) copy-start(bf16[4096,128]{1,0:T(8,128)(2,1)} %param.16) | copy-start | bytes 3145732
Sparse Core Ops, SparseCore 0:
  10.6 58.3 all-gather.8
  72.1 97.4 all-gather.10
  178.3 43.8 all-gather.14
  270.1 28.8 all-gather.16
  301.9 90.1 all-gather.12
where the time goes:
time: 773 us; the launch traced here: 762 us
  waiting for transfers between devices  336 us (43%)
  other arithmetic  270 us (35%)
  matrix products  60.9 us (8%)
  local copies, waits for them, and re-layouts  55.3 us (7%)
  between operations  19.8 us (3%)
  starting transfers between devices  14 us (2%)
    all_gather x3, waiting for transfers between devices, sent_together(): filled = lax.all_gather(both, axis, axis=dim, tiled=True)  249 us
    another operation x30, other arithmetic, local(): factor = jnp.linalg.cholesky(diag_block)  172 us
    another operation x3, other arithmetic, local(): jax.scipy.linalg.solve_triangular(factor, below_rows.T, lower=True)  85.5 us
    all_gather x1, waiting for transfers between devices, over_pieces(): tiles = lax.all_gather(x, axis)  41.6 us
    all_gather x1, waiting for transfers between devices, gathered_by_axis(): x = lax.all_gather(x, axis, axis=dim, tiled=True)  28.8 us
    another operation x14, matrix products, local(): factor = jnp.linalg.cholesky(diag_block)  23.3 us
    another operation x24, local copies, waits for them, and re-layouts  23 us
  transfers between devices with their start and end apart: 7, of which 7 were waited for; matrix products, arithmetic and copies ran while one was open for 1% of the time, Pallas kernels for 0%

commit v1 on v0

v1 whole, which is shorter than its diff:
```python
import jax
import jax.numpy as jnp
from jax import lax
from jax.experimental import pallas as pl
from jax.experimental.pallas import tpu as pltpu
from jax.sharding import PartitionSpec as P

HI = lax.Precision.HIGHEST
NB = 128

NZ, NX, NY, NC = 8, 4, 8, 2
DIMS = (NZ, NX, NY, NC)
MESH = pl.DeviceIdType.MESH


def add(a, b):
    return tuple((p + q) % n for p, q, n in zip(a, b, DIMS))


def neg(a):
    return tuple((-p) % n for p, n in zip(a, DIMS))


class Msg:
    def __init__(self, array, part, origin, off, dep, size):
        self.array, self.part, self.origin, self.off, self.dep, self.size = array, part, origin, off, dep, size


def ring(msgs, array, part, axis, start, dep, size, plus, minus):
    arrivals = []
    for step, hops in ((1, plus), (-1, minus)):
        unit = tuple(step if a == axis else 0 for a in range(4))
        unit = tuple(u % n for u, n in zip(unit, DIMS))
        origin, last = start, dep
        for _ in range(hops):
            m = Msg(array, part, origin, unit, last, size)
            msgs.append(m)
            origin = add(origin, neg(unit))
            arrivals.append((origin, m))
            last = m
    return arrivals


def ordered(msgs):
    import heapq
    free, done, pending = {}, {}, []
    followers = {}
    for n, m in enumerate(msgs):
        if m.dep is None:
            heapq.heappush(pending, (0.0, n))
        else:
            followers.setdefault(id(m.dep), []).append(n)
    while pending:
        at, n = heapq.heappop(pending)
        m = msgs[n]
        near = m.off == (0, 0, 0, 1)
        rate, hop = (250e3, 0.9) if near else (45e3, 1.7)
        begin = max(at, free.get(m.off, 0.0))
        free[m.off] = begin + m.size / rate
        done[n] = free[m.off] + hop
        for f in followers.get(id(m), []):
            heapq.heappush(pending, (done[n], f))
    return done


def position():
    r, c = lax.axis_index("rows"), lax.axis_index("cols")
    return (r // NX, lax.rem(r, NX), c // NC, lax.rem(c, NC))


def moved(me, off):
    return tuple(p if o == 0 else lax.rem(p + o, n) for p, o, n in zip(me, off, DIMS))


def device(me, off):
    z, x, y, k = moved(me, off)
    return {"rows": z * NX + x, "cols": y * NC + k}


def greet(me, offs):
    both = sorted(set(offs) | set(neg(o) for o in offs))
    barrier = pltpu.get_barrier_semaphore()
    for o in both:
        pl.semaphore_signal(barrier, inc=1, device_id=device(me, o), device_id_type=MESH)
    pl.semaphore_wait(barrier, len(both))


SPLIT = 80


def gather_messages(tsize, gsize, wrow, depth):
    msgs = []
    here = (0, 0, 0, 0)
    core = (0, 0, 0, 1)
    held = []
    for array, size, plus, minus in (("tok", tsize, 4, 3), ("cot", tsize, 3, 4), ("gp", gsize, 4, 3)):
        held += [(array, size, here, None)]
        held += [(array, size, o, m) for o, m in ring(msgs, array, 0, 2, here, None, size, plus, minus)]
    for array, size, o, m in held:
        msgs.append(Msg(array, 0, o, core, m, size))
    size = wrow * SPLIT
    got = [(here, None)] + ring(msgs, "w", 0, 0, here, None, size, 4, 3)
    for o, m in got:
        even = o[0] % 2 == 0
        ring(msgs, "w", 0, 1, o, m, size, 2 if even else 1, 1 if even else 2)
    size = wrow * (depth - SPLIT)
    got = [(here, None)] + ring(msgs, "w", 1, 1, here, None, size, 2, 1)
    for o, m in got:
        even = o[1] % 2 == 0
        ring(msgs, "w", 1, 0, o, m, size, 4 if even else 3, 3 if even else 4)
    return msgs


def gather_kernel(msgs, order, tok, cot, w, gp, tok_all, cot_all, w_all, gp_all, send, recv, own):
    me = position()
    depth, width, band = w.shape[0], tok.shape[1], gp.shape[0]

    def place(array, part, origin):
        z, x, y, k = moved(me, origin)
        if array == "w":
            at, rows = (0, SPLIT) if part == 0 else (SPLIT, depth - SPLIT)
            return w_all.at[pl.ds(pl.multiple_of((z * NX + x) * depth + at, 16), rows), :]
        c = y * NC + k
        if array == "gp":
            return gp_all.at[pl.ds(pl.multiple_of(c * band, 8), band), :]
        whole = tok_all if array == "tok" else cot_all
        return whole.at[:, pl.ds(pl.multiple_of(c * width, 128), width)]

    def mine(array, part):
        if array == "w":
            at, rows = (0, SPLIT) if part == 0 else (SPLIT, depth - SPLIT)
            return w.at[pl.ds(at, rows), :]
        return {"tok": tok, "cot": cot, "gp": gp}[array]

    def copy(n):
        m = msgs[n]
        src = mine(m.array, m.part) if m.origin == (0, 0, 0, 0) else place(m.array, m.part, m.origin)
        return pltpu.make_async_remote_copy(
            src_ref=src, dst_ref=place(m.array, m.part, m.origin), send_sem=send.at[n], recv_sem=recv.at[n],
            device_id=device(me, m.off), device_id_type=MESH)

    def arrived(n):
        m = msgs[n]
        there = place(m.array, m.part, add(m.origin, neg(m.off)))
        pltpu.make_async_remote_copy(
            src_ref=there, dst_ref=there, send_sem=send.at[n], recv_sem=recv.at[n],
            device_id=device(me, m.off), device_id_type=MESH).wait_recv()

    here = (0, 0, 0, 0)
    kept = [pltpu.make_async_copy(mine(a, p), place(a, p, here), own.at[i])
            for i, (a, p) in enumerate((("tok", 0), ("cot", 0), ("gp", 0), ("w", 0), ("w", 1)))]
    for c in kept:
        c.start()
    greet(me, [m.off for m in msgs])
    for n, m in enumerate(msgs):
        if m.dep is None:
            copy(n).start()
    for n in order:
        arrived(n)
        for f, m in enumerate(msgs):
            if m.dep is msgs[n]:
                copy(f).start()
    for n in range(len(msgs)):
        copy(n).wait_send()
    for c in kept:
        c.wait()


def gather(tok, cot, w, gp):
    msgs = gather_messages(tok.size * 2, gp.size * 4, w.shape[1] * 2, w.shape[0])
    times = ordered(msgs)
    order = sorted(range(len(msgs)), key=lambda n: (times[n], n))
    vm = pl.BlockSpec(memory_space=pltpu.VMEM)

    def body(*refs):
        gather_kernel(msgs, order, *refs)
    rows = NZ * NX
    cols = NY * NC
    return pl.pallas_call(
        body,
        out_shape=(
            jax.ShapeDtypeStruct((tok.shape[0], tok.shape[1] * cols), tok.dtype),
            jax.ShapeDtypeStruct((cot.shape[0], cot.shape[1] * cols), cot.dtype),
            jax.ShapeDtypeStruct((w.shape[0] * rows, w.shape[1]), w.dtype),
            jax.ShapeDtypeStruct((gp.shape[0] * cols, gp.shape[1]), gp.dtype)),
        in_specs=[vm] * 4, out_specs=(vm,) * 4,
        scratch_shapes=[pltpu.SemaphoreType.DMA((len(msgs),)), pltpu.SemaphoreType.DMA((len(msgs),)),
                        pltpu.SemaphoreType.DMA((5,))],
        compiler_params=pltpu.CompilerParams(collective_id=0, has_side_effects=True, vmem_limit_bytes=40 << 20),
        name="gather",
    )(tok, cot, w, gp)


def exchange_messages(size):
    msgs = []
    here = (0, 0, 0, 0)
    held = []
    got = [(here, None)] + ring(msgs, "d", 0, 0, here, None, size, 4, 3)
    for o, m in got:
        even = o[0] % 2 == 0
        held += [(0, o, m)] + [(0, p, q) for p, q in ring(msgs, "d", 0, 1, o, m, size, 2 if even else 1, 1 if even else 2)]
    got = [(here, None)] + ring(msgs, "d", 1, 1, here, None, size, 2, 1)
    for o, m in got:
        even = o[1] % 2 == 0
        held += [(1, o, m)] + [(1, p, q) for p, q in ring(msgs, "d", 1, 0, o, m, size, 4 if even else 3, 3 if even else 4)]
    for part, o, m in held:
        msgs.append(Msg("d", part, o, (0, 0, 0, 1), m, size))
    return msgs


HALF = 512
TAKE = 96
SUM_AT, SPREAD_AT, PANEL_AT = 8.0, 19.0, 27.0


def exchange_kernel(msgs, times, fp, dp, col_all, all3, d_all, d_other,
                    parts, hbuf, p3, dsend, drecv, s1, r1, s2, r2, sl, rl, s3, r3, s4, r4, own):
    me = position()
    r, c = lax.axis_index("rows"), lax.axis_index("cols")
    here, core = (0, 0, 0, 0), (0, 0, 0, 1)
    band = dp.shape[0]
    half = band // 2

    def rdma(src, dst, send, recv, to):
        return pltpu.make_async_remote_copy(src_ref=src, dst_ref=dst, send_sem=send, recv_sem=recv,
                                            device_id=to, device_id_type=MESH)

    def row_of(origin, part):
        z, x, _, _ = moved(me, origin)
        return pl.ds(pl.multiple_of((z * NX + x) * band + half * part, 8), half)

    def dcopy(n):
        m = msgs[n]
        src = dp.at[pl.ds(half * m.part, half), :] if m.origin == here else d_all.at[row_of(m.origin, m.part), :]
        if m.off == core:
            src = (dp.at[pl.ds(half * m.part, half), pl.ds(0, HALF)] if m.origin == here
                   else d_all.at[row_of(m.origin, m.part), pl.ds(0, HALF)])
            dst = d_other.at[row_of(m.origin, m.part), :]
        else:
            dst = d_all.at[row_of(m.origin, m.part), :]
        return rdma(src, dst, dsend.at[n], drecv.at[n], device(me, m.off))

    def darrived(n):
        m = msgs[n]
        if m.off == core:
            there = d_other.at[row_of(m.origin, m.part), :]
        else:
            there = d_all.at[row_of(add(m.origin, neg(m.off)), m.part), :]
        rdma(there, there, dsend.at[n], drecv.at[n], device(me, m.off)).wait_recv()

    cols_off = [(0, 0, dy, dk) for dy in range(NY) for dk in range(NC) if (dy, dk) != (0, 0)]
    rows_off = [(dz, dx, 0, 0) for dz in range(NZ) for dx in range(NX) if (dz, dx) != (0, 0)]
    y_off = [(0, 0, dy, 0) for dy in range(1, NY)]
    legs = [{"rows": 2 * c + e, "cols": r // 2} for e in range(2)]
    at_home = [jnp.logical_and(c == r // 2, lax.rem(r, 2) == e) for e in range(2)]

    def col_of(off):
        _, _, y, k = moved(me, off)
        return y * NC + k

    kept = pltpu.make_async_copy(dp, d_all.at[pl.ds(pl.multiple_of(r * band, 8), band), :], own)
    kept.start()
    both = sorted(set(cols_off + rows_off))
    barrier = pltpu.get_barrier_semaphore()
    for o in both:
        pl.semaphore_signal(barrier, inc=1, device_id=device(me, o), device_id_type=MESH)
    for e in range(2):
        @pl.when(jnp.logical_not(at_home[e]))
        def _():
            pl.semaphore_signal(barrier, inc=1, device_id=legs[e], device_id_type=MESH)
    pl.semaphore_wait(barrier, jnp.where(c == r // 2, len(both) + 1, len(both) + 2))

    first = [rdma(fp.at[col_of(o)], parts.at[i], s1.at[i], r1.at[i], device(me, o)) for i, o in enumerate(cols_off)]
    my_rows = pl.ds(pl.multiple_of(r * 16, 16), 16)
    second = [rdma(hbuf, col_all.at[my_rows, :], s2.at[i], r2.at[i], device(me, o)) for i, o in enumerate(rows_off)]
    leg_to = p3.at[pl.ds(pl.multiple_of(64 + lax.rem(r, 2) * 16, 16), 16), :]
    leg = [rdma(hbuf, leg_to, sl.at[e], rl.at[lax.rem(r, 2)], legs[e]) for e in range(2)]
    my_take = pl.ds(pl.multiple_of(c * TAKE, 8), TAKE)
    third = [rdma(p3, all3.at[my_take, :], s3.at[i], r3.at[i], device(me, o)) for i, o in enumerate(y_off)]

    def take_of(off):
        return all3.at[pl.ds(pl.multiple_of(col_of(off) * TAKE, 8), TAKE), :]

    def give(i):
        off = here if i == 0 else neg(y_off[i - 1])
        src = p3 if i == 0 else take_of(off)
        return rdma(src, take_of(off), s4.at[i], r4.at[i], device(me, core))

    def sum_up():
        total = fp[c]
        for i in range(len(cols_off)):
            first[i].wait_recv()
            total = total + parts[i]
        hbuf[...] = total
        col_all[my_rows, :] = total
        for e in range(2):
            @pl.when(jnp.logical_not(at_home[e]))
            def _():
                leg[e].start()

            @pl.when(at_home[e])
            def _():
                p3[pl.ds(64 + 16 * e, 16), :] = total
        for copy in second:
            copy.start()

    def spread():
        for i, o in enumerate(rows_off):
            z, x, _, _ = moved(me, neg(o))
            there = col_all.at[pl.ds(pl.multiple_of((z * NX + x) * 16, 16), 16), :]
            rdma(there, there, s2.at[i], r2.at[i], device(me, o)).wait_recv()
        for n in range(NZ * NX):
            p3[pl.ds(2 * n, 2), :] = col_all[pl.ds(16 * n, 2), :]
        for e in range(2):
            @pl.when(jnp.logical_not(at_home[e]))
            def _():
                there = p3.at[pl.ds(64 + 16 * e, 16), :]
                rdma(there, there, sl.at[e], rl.at[e], legs[e]).wait_recv()
        all3[my_take, :] = p3[...]
        for copy in third:
            copy.start()
        give(0).start()

    def panel():
        for i, o in enumerate(y_off):
            there = take_of(neg(o))
            rdma(there, there, s3.at[i], r3.at[i], device(me, o)).wait_recv()
            give(i + 1).start()

    for copy in first:
        copy.start()
    for n, m in enumerate(msgs):
        if m.dep is None:
            dcopy(n).start()
    events = sorted([(times[n], n) for n in range(len(msgs))]
                    + [(SUM_AT, -1), (SPREAD_AT, -2), (PANEL_AT, -3)])
    for _, n in events:
        if n < 0:
            (sum_up, spread, panel)[-n - 1]()
            continue
        darrived(n)
        for f, m in enumerate(msgs):
            if m.dep is msgs[n]:
                dcopy(f).start()
    for i in range(NY):
        off = here if i == 0 else neg(y_off[i - 1])
        there = take_of(add(off, core))
        rdma(there, there, s4.at[i], r4.at[i], device(me, core)).wait_recv()
    for n in range(len(msgs)):
        dcopy(n).wait_send()
    for copy in first + second + third:
        copy.wait_send()
    for e in range(2):
        @pl.when(jnp.logical_not(at_home[e]))
        def _():
            leg[e].wait_send()
    for i in range(NY):
        give(i).wait_send()
    kept.wait()


def exchange(fp, dp):
    msgs = exchange_messages(dp.size * 2)
    times = ordered(msgs)
    vm = pl.BlockSpec(memory_space=pltpu.VMEM)
    f32 = jnp.float32
    rows, cols = NZ * NX, NY * NC
    dma = pltpu.SemaphoreType.DMA

    def body(*refs):
        exchange_kernel(msgs, times, *refs)
    return pl.pallas_call(
        body,
        out_shape=(
            jax.ShapeDtypeStruct((rows * 16, 128), f32),
            jax.ShapeDtypeStruct((cols * TAKE, 128), f32),
            jax.ShapeDtypeStruct((rows * dp.shape[0], dp.shape[1]), f32),
            jax.ShapeDtypeStruct((rows * dp.shape[0], HALF), f32)),
        in_specs=[vm] * 2, out_specs=(vm,) * 4,
        scratch_shapes=[
            pltpu.VMEM((cols - 1, 16, 128), f32), pltpu.VMEM((16, 128), f32), pltpu.VMEM((TAKE, 128), f32),
            dma((len(msgs),)), dma((len(msgs),)), dma((cols - 1,)), dma((cols - 1,)), dma((rows - 1,)), dma((rows - 1,)),
            dma((2,)), dma((2,)), dma((NY - 1,)), dma((NY - 1,)), dma((NY,)), dma((NY,)), dma],
        compiler_params=pltpu.CompilerParams(collective_id=1, has_side_effects=True, vmem_limit_bytes=40 << 20),
        name="exchange",
    )(fp, dp)


def lanes(x, j):
    return jnp.broadcast_to(x[:, j:j + 1], x.shape)


def subl(x, k):
    return jnp.broadcast_to(x[k:k + 1, :], x.shape)


def factor_block(A, V):
    n = len(A)
    A = list(A); V = list(V)
    sub = lax.broadcasted_iota(jnp.int32, (8, NB), 0)
    for p in range(n):
        a, v = A[p], V[p]
        C = [lanes(a, 8 * p + j) for j in range(8)]
        Us, Vs, R, S = [], [], [], []
        for k in range(8):
            d = subl(C[k], k)
            r = lax.rsqrt(d)
            sb = [subl(C[k], j) if j > k else None for j in range(8)]
            rd = r * r
            Cs = C[k] * rd
            for j in range(k + 1, 8):
                C[j] = C[j] - Cs * sb[j]
            R.append(r)
            S.append([None if s is None else s * r for s in sb])
            uk = subl(a, k) * r
            vk = subl(v, k) * r
            m = jnp.where(sub > k, C[k] * r, 0.0)
            a = a - m * uk
            v = v - m * vk
            Us.append(uk); Vs.append(vk)
        un, vn = Us[0], Vs[0]
        for k in range(1, 8):
            un = jnp.where(sub == k, Us[k], un)
            vn = jnp.where(sub == k, Vs[k], vn)
        A[p], V[p] = un, vn
        for q in range(p + 1, n):
            aq, vq = A[q], V[q]
            if q == p + 1:
                G = [lanes(aq, 8 * p + j) for j in range(8)]
                L = []
                for k in range(8):
                    t = G[k]
                    for m in range(k):
                        t = t - L[m] * S[m][k]
                    L.append(t * R[k])
                for k in range(8):
                    aq = aq - L[k] * Us[k]
                    vq = vq - L[k] * Vs[k]
            else:
                for k in range(8):
                    l = lanes(aq, 8 * p + k) * R[k]
                    aq = aq - l * Us[k]
                    vq = vq - l * Vs[k]
            A[q], V[q] = aq, vq
    return A, V


def factor_kernel(x, y, gp, f0, frow, u_ref, inv_ref):
    n = u_ref.shape[0]
    nb = n // NB
    seqs = f0.shape[0]
    r = lax.axis_index("rows")
    k = lax.rem(lax.axis_index("cols"), NC)
    own = seqs // (NZ * NX)
    heads = 16
    lane = lax.broadcasted_iota(jnp.int32, (seqs, 256), 1)
    seq = lax.broadcasted_iota(jnp.int32, (seqs, 256), 0)
    pick = jnp.where(jnp.logical_and(lane >= heads, lane < heads + own), jnp.where(seq == own * r + lane - heads, 1.0, 0.0), 0.0)
    z = jnp.where(lane < 32, pick, frow[...] * (1.0 / seqs))
    row = lax.broadcasted_iota(jnp.int32, (8, NB), 0)
    col = lax.broadcasted_iota(jnp.int32, (8, NB), 1)
    tdot = lambda a, b: lax.dot_general(a, b, (((0,), (0,)), ((), ())), precision=HI, preferred_element_type=jnp.float32)

    for b in range(nb):
        rows = pl.ds(b * NB, NB)
        u_ref[rows, pl.ds(pl.multiple_of(k * HALF, HALF), HALF)] = x[rows, :HALF]
        u_ref[rows, pl.ds(pl.multiple_of((1 - k) * HALF, HALF), HALF)] = y[rows, :]
        lhs = f0[:, b * NB:(b + 1) * NB]
        u_ref[rows, :n] = u_ref[rows, :n] + tdot(lhs, f0[...]) * (1.0 / seqs)
        low = lane[:NB, :NB]
        base = jnp.where(low < heads, x[rows, HALF:], jnp.where(low < 32, 0.0, gp[rows, :NB]))
        extra = tdot(lhs, z)
        u_ref[rows, n:n + NB] = base + extra[:, :NB]
        u_ref[rows, n + NB:] = gp[rows, NB:] + extra[:, NB:]

    def outer(b, _):
        o = pl.multiple_of(b * NB, NB)
        A = [u_ref[pl.ds(o + 8 * p, 8), pl.ds(o, NB)] for p in range(16)]
        V = [jnp.where(col == row + 8 * p, 1.0, 0.0) for p in range(16)]
        A, V = factor_block(A, V)
        for p in range(16):
            inv_ref[pl.ds(8 * p, 8), :] = V[p]
        u_ref[pl.ds(o, NB), :] = jnp.dot(inv_ref[...], u_ref[pl.ds(o, NB), :], precision=HI, preferred_element_type=jnp.float32)
        for p in range(16):
            u_ref[pl.ds(o + 8 * p, 8), pl.ds(o, NB)] = jnp.where(col >= row + 8 * p, A[p], 0.0)

        def trail(q, _):
            oq = pl.multiple_of(q * NB, NB)
            lhs = u_ref[pl.ds(o, NB), pl.ds(oq, NB)]
            u_ref[pl.ds(oq, NB), :] = u_ref[pl.ds(oq, NB), :] - tdot(lhs, u_ref[pl.ds(o, NB), :])
            return 0
        lax.fori_loop(b + 1, nb, trail, 0)
        return 0
    lax.fori_loop(0, nb, outer, 0)


def factored(x, y, gp, f0, frow):
    n = x.shape[0]
    vm = pl.BlockSpec(memory_space=pltpu.VMEM)
    return pl.pallas_call(
        factor_kernel,
        out_shape=jax.ShapeDtypeStruct((n, n + 256), jnp.float32),
        in_specs=[vm] * 5, out_specs=vm,
        scratch_shapes=[pltpu.VMEM((NB, NB), jnp.float32)],
        compiler_params=pltpu.CompilerParams(vmem_limit_bytes=40 << 20),
        name="factor",
    )(x, y, gp, f0, frow)


def local(tokens, cotangent, gate_weight, down_weight, proj_in, proj_out, lengths, loss_mask, gram_in, queries):
    f32 = jnp.float32
    r, c = lax.axis_index("rows"), lax.axis_index("cols")
    k = lax.rem(c, NC)
    cycles, band_rows, _, band_cols = gram_in.shape
    seq_count, window = loss_mask.shape
    hidden = gate_weight.shape[1]
    rows, cols = NZ * NX, NY * NC
    seqs = seq_count * rows
    pw = band_rows * rows

    weights = jnp.concatenate([gate_weight, down_weight], axis=1)
    band = gram_in[:, :, 0, :].reshape(cycles * band_rows, band_cols).T
    tok, cot, wts, gp = gather(tokens, cotangent, weights, band)

    diag = gp[:, :band_rows].T
    diag = lax.dynamic_slice_in_dim(diag, k * HALF, HALF, 1)
    head = jnp.pad(queries[:, 0, :].T, ((0, 0), (0, 128 - queries.shape[0])))
    dp = jnp.concatenate([diag, head], axis=1)

    gate_pre = jnp.dot(tok, wts[:, :512], preferred_element_type=f32)[:, :hidden]
    grad_hidden = jnp.dot(cot, wts[:, 384:], preferred_element_type=f32)[:, hidden - 384:]
    grad_up = (grad_hidden * jax.nn.silu(gate_pre)).astype(jnp.bfloat16)
    outer = jnp.dot(grad_up, proj_out, preferred_element_type=f32)
    inner = jnp.dot(tok, proj_in, preferred_element_type=f32)
    positions = jnp.arange(window, dtype=jnp.int32)
    live = (positions[None, :] >= (window - lengths)[:, None]).astype(f32) * loss_mask.astype(f32)
    weighted = inner.reshape(seq_count, window, -1) * live[:, :, None]
    feats = jnp.einsum("stk,stl->skl", weighted, outer.reshape(seq_count, window, -1), precision=HI)
    width = feats.shape[2]
    fp = feats.reshape(seq_count, cycles, cols, width).transpose(2, 1, 0, 3).reshape(cols, 16, 128)

    col_all, all3, d_own, d_other = exchange(fp, dp)

    fcol = col_all.reshape(rows, cycles, seq_count, width).transpose(0, 2, 1, 3).reshape(seqs, cycles * width)
    take = all3.reshape(cols, TAKE, 128)
    f0 = take[:, :64].reshape(cols, seqs, width).transpose(1, 0, 2).reshape(seqs, cols * width)
    frow = take[:, 64:].reshape(cols, 2, cycles, seq_count, width)
    frow = lax.dynamic_slice_in_dim(frow, lax.rem(r, 2) * band_rows, band_rows, 4)
    frow = frow.transpose(0, 1, 3, 2, 4).reshape(seqs, cycles * band_rows)

    u = factored(d_own, d_other, gp, f0, frow)

    update = lax.dot_general(frow, fcol, (((0,), (0,)), ((), ())), precision=HI, preferred_element_type=f32) / seqs
    updated = gram_in + update.reshape(cycles, band_rows, cycles, band_cols)
    strip = lax.dynamic_slice_in_dim(u, c * band_cols, band_cols, 0)
    tile = lax.dynamic_slice_in_dim(strip, r * band_rows, band_rows, 1)
    at_row = lax.broadcasted_iota(jnp.int32, tile.shape, 1) + r * band_rows
    at_col = lax.broadcasted_iota(jnp.int32, tile.shape, 0) + c * band_cols
    tile = jnp.where(at_row >= at_col, tile, 0.0)
    strip = jnp.concatenate([tile, strip[:, pw + band_rows:]], axis=1)
    panel = strip.T.reshape(cycles, band_rows, 1, band_cols)
    gram_next = jnp.concatenate([panel, updated[:, :, 1:]], axis=2)

    count = queries.shape[0]
    extra = u[:, pw:]
    solved = extra[:, :count]
    both = lax.dot_general(solved, extra, (((0,), (0,)), ((), ())), precision=HI, preferred_element_type=f32)
    scores = both[:, count:count + seq_count]
    tail = queries[:, 1:] - both[:, band_rows:].reshape(count, cycles - 1, band_rows)
    own = lax.dynamic_slice_in_dim(solved, r * band_rows, band_rows, 0).T
    query_next = jnp.concatenate([own[:, None], tail], axis=1)
    return gram_next, query_next, scores


def solution(mesh):
    return jax.shard_map(
        local,
        mesh=mesh,
        in_specs=(
            P("rows", "cols"), P("rows", "cols"), P("rows", "cols"), P("rows", "cols"), P(), P("cols", None),
            P("rows"), P("rows", None), P(None, "rows", None, "cols"), P("cols", None, "rows")),
        out_specs=(P(None, "rows", None, "cols"), P("cols", None, "rows"), P("cols", "rows")),
        check_vma=False,
    )
```

time: 773 us -> 269 us (0.35); the launches traced: 762 us -> 268 us
  waiting for transfers between devices: 336 us -> 0 us
  other arithmetic: 270 us -> 7.1 us
  Pallas kernels: 0 us -> 210 us
  matrix products: 60.9 us -> 15.1 us
  local copies, waits for them, and re-layouts: 55.3 us -> 34.9 us
  between operations: 19.8 us -> 1.02 us
  starting transfers between devices: 14 us -> 0 us
    all_gather x5 -> x0, waiting for transfers between devices: 319 us -> none  [the longest x3 249 us: sent_together(): filled = lax.all_gather(both, axis, axis=dim, tiled=True)]
    another operation x33 -> x0, other arithmetic: 258 us -> none  [the longest x30 172 us: local(): factor = jnp.linalg.cholesky(diag_block)]
    pallas_call x0 -> x3, Pallas kernels: none -> 210 us  [the longest x1 96.5 us: factored(): pl.pallas_call(factor_kernel, out_shape=jax.ShapeDtypeStruct((n, n + 256)...]
    another operation x59 -> x0, matrix products: 47.2 us -> none  [the longest x14 23.3 us: local(): factor = jnp.linalg.cholesky(diag_block)]
    another operation x38 -> x1, local copies, waits for them, and re-layouts: 27.4 us -> 0.08 us  [local(): band = gram_in[:, :, 0, :].reshape(cycles * band_rows, band_cols).T]
    all_to_all x2 -> x0, waiting for transfers between devices: 16.6 us -> none  [the longest x1 8.46 us: copy_for_each(): lax.all_to_all(jnp.broadcast_to(x[None], (size, *x.shape)), axis, 0, 0, t...]
    all_to_all x2 -> x0, starting transfers between devices: 13.8 us -> none  [the longest x1 9.9 us: local(): lax.all_to_all(by_owner, 'rows', split_axis=2, concat_axis=0, tiled=True)]
    unnamed x35 -> x34, local copies, waits for them, and re-layouts: 13 us -> 18 us
  transfers between devices with their start and end apart: 7 -> 0, of which waited for: 7 -> 0; matrix products, arithmetic and copies ran while one was open for 1% -> 0% of each run, Pallas kernels for 0% -> 0%
where the time goes in v1:
time: 269 us; the launch traced here: 268 us
  Pallas kernels  210 us (78%)
  local copies, waits for them, and re-layouts  34.9 us (13%)
  matrix products  15.1 us (6%)
  other arithmetic  7.1 us (3%)
    pallas_call x1, Pallas kernels, factored(): pl.pallas_call(factor_kernel, out_shape=jax.ShapeDtypeStruct((n, n + 256)...  96.5 us
    pallas_call x1, Pallas kernels, gather(): pl.pallas_call(body, out_shape=(jax.ShapeDtypeStruct((tok.shape[0], tok.s...  61.8 us
    pallas_call x1, Pallas kernels, exchange(): pl.pallas_call(body, out_shape=(jax.ShapeDtypeStruct((rows * 16, 128), f3...  51.4 us
    unnamed x34, local copies, waits for them, and re-layouts  18 us
    dot_general x1, matrix products, local(): outer = jnp.dot(grad_up, proj_out, preferred_element_type=f32)  6.53 us

profile of v1, /device:TPU:1, one launch (start us, length us, event | category | flops | bytes accessed | tf_op | source)
XLA Modules:
  0.0 267.8 jit_solution(31746264624091807)
XLA Ops:
  0.6 0.0 copy-start
  0.6 1.1 copy.24
  1.7 1.0 copy.23
  2.7 0.1 pad_maximum_fusion.1.refs_2_
  2.9 1.3 slice.49
  4.2 0.1 copy.25
  4.3 0.0 copy-start.7
  4.3 0.9 copy-done.7
  5.2 0.9 copy-done.8
  6.1 61.8 %gather.1 = (bf16[256,4096]{1,0:T(8,128)(2,1)S(1)}, bf16[256,4096]{1,0:T(8,128)(2,1)S(1)}, bf16[4096,896]{1,0:T(8,128)(2,1)S(1)}, f32[1024,256]{1,0:T(8,128)S(1)}) custom-call(bf16[256,256]{1,0:T(8,128)(2,1)S(1)} %copy-done.7, bf16[256,256]{1,0:T(8,128)(2,1)S(1)} %copy-done.8, bf16[128,896]{1,0:T(8,128)(2,1)S(1)} %pad_maximum_fusion.1.refs_2_, ...), custom_call_target="tpu_custom_call" | custom-call | tf_op jit(solution)/shard_map/gather/pallas_call | solution.py:179
  67.8 0.0 copy-start.10
  67.9 1.3 copy-done.10
  69.2 1.4 copy-done.4
  70.6 2.2 copy-done.9
  72.8 1.7 fusion
  74.4 0.0 copy-done.13
  74.5 0.0 copy-start.14
  74.5 0.0 copy-start.12
  74.5 6.5 %fusion.11 = f32[256,64]{0,1:T(8,128)S(1)} fusion(bf16[448,64]{0,1:T(8,128)(2,1)S(1)} %copy-done.13, bf16[256,4096]{1,0:T(8,128)(2,1)} %copy-done.10, bf16[4096,896]{1,0:T(8,128)(2,1)} %copy-done.9, f32[256,448]{0,1:T(8,128)S(1)} %fusion), kind=kOutput, calls=%fused_computation.7 | convolution fusion | flops 954892288 | bytes 6873088 | tf_op jit(solution)/shard_map/dot_general | solution.py:533
  81.0 0.0 slice-start.1
  81.0 0.1 reshape.51
  81.2 2.3 fusion.27
  83.5 0.1 convert_select_fusion
  83.5 0.7 fusion.21
  84.2 0.2 copy.28
  84.4 0.1 reshape.53.refs_0_
  84.5 0.1 copy.40
  84.6 0.3 copy.29
  85.0 51.4 %exchange.1 = (f32[512,128]{1,0:T(8,128)S(1)}, f32[1536,128]{1,0:T(8,128)S(1)}, f32[1024,640]{1,0:T(8,128)S(1)}, f32[1024,512]{1,0:T(8,128)S(1)}) custom-call(f32[16,16,128]{2,1,0:T(8,128)S(1)} %reshape.53.refs_0_, f32[32,640]{1,0:T(8,128)S(1)} %select_maximum_fusion.refs_1_), custom_call_target="tpu_custom_call" | custom-call | tf_op jit(solution)/shard_map/exchange/pallas_call | solution.py:372
  136.5 1.5 copy-done.2
  138.0 1.3 copy-done.5
  139.3 0.7 slice.71
  140.0 2.0 reshape.57
  142.0 1.4 dynamic-slice_bitcast_fusion
  143.4 0.8 copy.32
  144.2 1.2 reshape.58.frow
  145.5 1.0 reshape.60
  146.5 1.1 copy.44
  147.6 0.9 reshape.61
  148.4 1.6 convolution_multiply_fusion
  150.0 1.2 reshape.62
  151.2 2.7 %slice_add_fusion = f32[8,32,7,64]{3,2,1,0:T(8,128)} fusion(f32[8,32,8,64]{3,2,1,0:T(8,128)} %reshape.62, f32[8,32,8,64]{3,2,1,0:T(8,128)} %param.18), kind=kLoop, calls=%fused_computation.10 | loop fusion | flops 114688 | bytes 1376256 | tf_op jit(solution)/shard_map/add | solution.py:554
  154.0 1.2 reshape.55
  155.1 1.5 copy.31
  156.7 0.2 copy.33.f0
  156.9 0.0 copy-start.3
  156.9 1.7 copy-done.3
  158.6 1.6 copy-done.6
  160.2 96.5 %factor.1 = f32[1024,1280]{1,0:T(8,128)S(1)} custom-call(f32[1024,640]{1,0:T(8,128)S(1)} %copy-done.3, f32[1024,512]{1,0:T(8,128)S(1)} %copy-done.6, f32[1024,256]{1,0:T(8,128)S(1)} %get-tuple-element.14.gp, f32[128,1024]{1,0:T(8,128)S(1)} %copy.33.f0, f32[128,256]{1,0:T(8,128)S(1)} %reshape.58.frow), custom_call_target="tpu_custom_call" | custom-call | tf_op jit(solution)/shard_map/factor/pallas_call | solution.py:500
  256.8 2.3 copy-done.1
  259.1 1.0 dynamic-slice.4
  260.1 1.0 dynamic-slice_select_fusion
  261.1 0.1 maximum_bitcast_fusion
  261.2 0.1 copy.34
  261.3 2.5 pad_maximum_fusion
  263.7 2.3 fusion.13
  266.1 0.1 slice.76
  266.2 0.1 reshape.63
  266.3 0.0 copy-done.11
  266.3 0.0 slice-done
  266.3 0.1 copy.37
  266.4 0.7 pad_maximum_fusion.2
  267.0 0.1 slice.77
  267.1 0.7 copy.38
  (23 shorter events, 0.1 us)
Async XLA Ops:
  0.6 80.5 %copy-start = (bf16[4096,128]{1,0:T(8,128)(2,1)S(1)}, bf16[4096,128]{1,0:T(8,128)(2,1)}, u32[]{:S(2)}) copy-start(bf16[4096,128]{1,0:T(8,128)(2,1)} %param.14) | copy-start | bytes 3145732
  4.3 0.9 copy-start.7
  5.2 0.9 copy-start.8
  67.8 1.3 copy-start.10
  69.2 1.4 copy-start.4
  69.2 3.6 %copy-start.9 = (bf16[4096,896]{1,0:T(8,128)(2,1)}, bf16[4096,896]{1,0:T(8,128)(2,1)S(1)}, u32[]{:S(2)}) copy-start(bf16[4096,896]{1,0:T(8,128)(2,1)S(1)} %get-tuple-element.13) | copy-start | bytes 22020100
  69.2 5.3 %copy-start.13 = (bf16[448,64]{0,1:T(8,128)(2,1)S(1)}, bf16[448,64]{0,1:T(8,128)(2,1)}, u32[]{:S(2)}) copy-start(bf16[448,64]{0,1:T(8,128)(2,1)} %param.15) | copy-start | bytes 172036
  74.5 9.0 %copy-start.14 = (s32[4]{0:T(128)S(1)}, s32[4]{0:T(128)}, u32[]{:S(2)}) copy-start(s32[4]{0:T(128)} %param.16) | copy-start | bytes 52
  74.5 9.0 %copy-start.12 = (s32[4,64]{1,0:T(4,128)S(1)}, s32[4,64]{1,0:T(4,128)}, u32[]{:S(2)}) copy-start(s32[4,64]{1,0:T(4,128)} %param.17) | copy-start | bytes 3076
  81.0 3.5 %slice-start.1 = ((f32[16,8,32]{2,1,0:T(8,128)}), f32[16,1,32]{2,1,0:T(1,128)S(1)}, s32[]{:S(2)}) async-start(f32[16,8,32]{2,1,0:T(8,128)} %param.19), calls=%async_computation.1 | async-start | bytes 16384 | tf_op jit(solution)/shard_map/slice | solution.py:527
  136.5 1.5 copy-start.2
  138.0 1.3 copy-start.5
  156.9 1.7 copy-start.3
  158.6 1.6 copy-start.6
  256.8 2.3 copy-start.1
  259.1 7.2 %copy-start.11 = (f32[16,8,32]{2,1,0:T(8,128)S(1)}, f32[16,8,32]{2,1,0:T(8,128)}, u32[]{:S(2)}) copy-start(f32[16,8,32]{2,1,0:T(8,128)} %param.19) | copy-start | bytes 49156
  259.1 7.2 %slice-start = ((f32[1024,1280]{1,0:T(8,128)}), f32[1024,16]{1,0:T(8,128)S(1)}, s32[]{:S(2)}) async-start(f32[1024,1280]{1,0:T(8,128)} %copy-done.1), calls=%async_computation | async-start | bytes 1048576 | tf_op jit(solution)/shard_map/slice | solution.py:566

commit v2 on v1

--- a/solution.py
+++ b/solution.py
@@ -186,7 +186,7 @@
         in_specs=[vm] * 4, out_specs=(vm,) * 4,
         scratch_shapes=[pltpu.SemaphoreType.DMA((len(msgs),)), pltpu.SemaphoreType.DMA((len(msgs),)),
                         pltpu.SemaphoreType.DMA((5,))],
-        compiler_params=pltpu.CompilerParams(collective_id=0, has_side_effects=True, vmem_limit_bytes=40 << 20),
+        compiler_params=pltpu.CompilerParams(collective_id=0, has_side_effects=True, vmem_limit_bytes=4 << 20),
         name="gather",
     )(tok, cot, w, gp)
 
@@ -210,7 +210,7 @@
 
 HALF = 512
 TAKE = 96
-SUM_AT, SPREAD_AT, PANEL_AT = 8.0, 19.0, 27.0
+SUM_AT, SPREAD_AT, PANEL_AT = 6.0, 10.0, 19.0
 
 
 def exchange_kernel(msgs, times, fp, dp, col_all, all3, d_all, d_other,
@@ -309,8 +309,8 @@
             z, x, _, _ = moved(me, neg(o))
             there = col_all.at[pl.ds(pl.multiple_of((z * NX + x) * 16, 16), 16), :]
             rdma(there, there, s2.at[i], r2.at[i], device(me, o)).wait_recv()
-        for n in range(NZ * NX):
-            p3[pl.ds(2 * n, 2), :] = col_all[pl.ds(16 * n, 2), :]
+        for n in range(2 * NZ * NX):
+            p3[pl.ds(n, 1), :] = col_all[pl.ds(8 * n, 1), :]
         for e in range(2):
             @pl.when(jnp.logical_not(at_home[e]))
             def _():
@@ -381,7 +381,7 @@
             pltpu.VMEM((cols - 1, 16, 128), f32), pltpu.VMEM((16, 128), f32), pltpu.VMEM((TAKE, 128), f32),
             dma((len(msgs),)), dma((len(msgs),)), dma((cols - 1,)), dma((cols - 1,)), dma((rows - 1,)), dma((rows - 1,)),
             dma((2,)), dma((2,)), dma((NY - 1,)), dma((NY - 1,)), dma((NY,)), dma((NY,)), dma],
-        compiler_params=pltpu.CompilerParams(collective_id=1, has_side_effects=True, vmem_limit_bytes=40 << 20),
+        compiler_params=pltpu.CompilerParams(collective_id=1, has_side_effects=True, vmem_limit_bytes=4 << 20),
         name="exchange",
     )(fp, dp)
 
@@ -394,38 +394,35 @@
     return jnp.broadcast_to(x[k:k + 1, :], x.shape)
 
 
-def factor_block(A, V):
+def factor_block(A, V, group=8):
     n = len(A)
-    A = list(A); V = list(V)
+    A, V = list(A), list(V)
     sub = lax.broadcasted_iota(jnp.int32, (8, NB), 0)
-    for p in range(n):
-        a, v = A[p], V[p]
-        C = [lanes(a, 8 * p + j) for j in range(8)]
-        Us, Vs, R, S = [], [], [], []
-        for k in range(8):
-            d = subl(C[k], k)
-            r = lax.rsqrt(d)
-            sb = [subl(C[k], j) if j > k else None for j in range(8)]
-            rd = r * r
-            Cs = C[k] * rd
-            for j in range(k + 1, 8):
-                C[j] = C[j] - Cs * sb[j]
-            R.append(r)
-            S.append([None if s is None else s * r for s in sb])
-            uk = subl(a, k) * r
-            vk = subl(v, k) * r
-            m = jnp.where(sub > k, C[k] * r, 0.0)
-            a = a - m * uk
-            v = v - m * vk
-            Us.append(uk); Vs.append(vk)
-        un, vn = Us[0], Vs[0]
-        for k in range(1, 8):
-            un = jnp.where(sub == k, Us[k], un)
-            vn = jnp.where(sub == k, Vs[k], vn)
-        A[p], V[p] = un, vn
-        for q in range(p + 1, n):
-            aq, vq = A[q], V[q]
-            if q == p + 1:
+    for g in range(0, n, group):
+        for p in range(g, g + group):
+            a, v = A[p], V[p]
+            C = [lanes(a, 8 * p + j) for j in range(8)]
+            Us, Vs, R, S = [], [], [], []
+            for k in range(8):
+                r = lax.rsqrt(subl(C[k], k))
+                sb = [subl(C[k], j) if j > k else None for j in range(8)]
+                Cs = C[k] * (r * r)
+                for j in range(k + 1, 8):
+                    C[j] = C[j] - Cs * sb[j]
+                R.append(r)
+                S.append([None if t is None else t * r for t in sb])
+                uk, vk = subl(a, k) * r, subl(v, k) * r
+                m = jnp.where(sub > k, C[k] * r, 0.0)
+                a, v = a - m * uk, v - m * vk
+                Us.append(uk)
+                Vs.append(vk)
+            un, vn = Us[0], Vs[0]
+            for k in range(1, 8):
+                un = jnp.where(sub == k, Us[k], un)
+                vn = jnp.where(sub == k, Vs[k], vn)
+            A[p], V[p] = un, vn
+            for q in range(p + 1, g + group):
+                aq, vq = A[q], V[q]
                 G = [lanes(aq, 8 * p + j) for j in range(8)]
                 L = []
                 for k in range(8):
@@ -434,77 +431,197 @@
                         t = t - L[m] * S[m][k]
                     L.append(t * R[k])
                 for k in range(8):
-                    aq = aq - L[k] * Us[k]
-                    vq = vq - L[k] * Vs[k]
-            else:
-                for k in range(8):
-                    l = lanes(aq, 8 * p + k) * R[k]
-                    aq = aq - l * Us[k]
-                    vq = vq - l * Vs[k]
-            A[q], V[q] = aq, vq
+                    aq, vq = aq - L[k] * Us[k], vq - L[k] * Vs[k]
+                A[q], V[q] = aq, vq
+        if g + group < n:
+            ug = jnp.concatenate(A[g:g + group], 0)
+            vg = jnp.concatenate(V[g:g + group], 0)
+            change = tdot(ug, jnp.concatenate([ug, vg], 1), HI)
+            for q in range(g + group, n):
+                A[q] = A[q] - change[8 * q:8 * q + 8, :NB]
+                V[q] = V[q] - change[8 * q:8 * q + 8, NB:]
     return A, V
 
 
-def factor_kernel(x, y, gp, f0, frow, u_ref, inv_ref):
-    n = u_ref.shape[0]
-    nb = n // NB
-    seqs = f0.shape[0]
-    r = lax.axis_index("rows")
-    k = lax.rem(lax.axis_index("cols"), NC)
-    own = seqs // (NZ * NX)
+def split3(x):
+    h = x.astype(jnp.bfloat16)
+    rest = x - h.astype(jnp.float32)
+    m = rest.astype(jnp.bfloat16)
+    return h, m, (rest - m.astype(jnp.float32)).astype(jnp.bfloat16)
+
+
+def tdot(a, b, precision=None):
+    return lax.dot_general(a, b, (((0,), (0,)), ((), ())), precision=precision, preferred_element_type=jnp.float32)
+
+
+def paired(even, odd, lane):
+    return jnp.where(lane < 64, even, pltpu.roll(odd, 64, 1)), jnp.where(lane < 64, pltpu.roll(even, 64, 1), odd)
+
+
+def factor_kernel(x, y, gp, all3, col_all, upd, both, strip, own, u, inv, hh, hm, ml, mh, rowp, frow, fcol):
+    n, width = u.shape
+    nb, half = n // NB, n // 2
+    r, c = lax.axis_index("rows"), lax.axis_index("cols")
+    k = lax.rem(c, NC)
+    cols = NY * NC
+    seqs = 128
+    per = seqs // (NZ * NX)
     heads = 16
-    lane = lax.broadcasted_iota(jnp.int32, (seqs, 256), 1)
-    seq = lax.broadcasted_iota(jnp.int32, (seqs, 256), 0)
-    pick = jnp.where(jnp.logical_and(lane >= heads, lane < heads + own), jnp.where(seq == own * r + lane - heads, 1.0, 0.0), 0.0)
-    z = jnp.where(lane < 32, pick, frow[...] * (1.0 / seqs))
+    lane64 = lax.broadcasted_iota(jnp.int32, (64, NB), 1)
+
+    def keep(h, m, l, cs):
+        hh[pl.ds(0, NB), cs] = h
+        hh[pl.ds(NB, NB), cs] = h
+        hm[pl.ds(0, NB), cs] = h
+        hm[pl.ds(NB, NB), cs] = m
+        ml[pl.ds(0, NB), cs] = m
+        ml[pl.ds(NB, NB), cs] = l
+        mh[pl.ds(0, NB), cs] = m
+        mh[pl.ds(NB, NB), cs] = h
+
+    def product(qs, cs):
+        return tdot(hh[:, qs], hm[:, cs]) + (tdot(ml[:, qs], hh[:, cs]) + tdot(mh[:, qs], ml[:, cs]))
+
+    for p in range(cols // 2):
+        top, low = paired(all3[pl.ds(2 * p * TAKE, 64), :], all3[pl.ds((2 * p + 1) * TAKE, 64), :], lane64)
+        keep(*split3(jnp.concatenate([top, low], 0)), pl.ds(p * NB, NB))
+    for p in range(cols):
+        rowp[pl.ds(32 * p, 32), :] = all3[pl.ds(p * TAKE + 64, 32), :]
+    for p in range(4):
+        top, low = paired(col_all[pl.ds(2 * p, 64, stride=8), :], col_all[pl.ds(2 * p + 1, 64, stride=8), :], lane64)
+        fcol[pl.ds(0, 64), pl.ds(p * NB, NB)] = top
+        fcol[pl.ds(64, 64), pl.ds(p * NB, NB)] = low
+    second = lax.rem(r, 2) == 1
+    for t in range(2):
+        top = low = jnp.zeros((64, NB), jnp.float32)
+        for q in range(4):
+            piece = rowp[pl.ds(4 * t + q, 64, stride=8), :]
+            piece = jnp.where(second, pltpu.roll(piece, 96, 1), piece)
+            here = lane64 // 32 == q
+            top = jnp.where(here, piece if q == 0 else pltpu.roll(piece, 32 * q, 1), top)
+            low = jnp.where(here, piece if q == 2 else pltpu.roll(piece, (32 * q + 64) % 128, 1), low)
+        frow[pl.ds(0, 64), pl.ds(t * NB, NB)] = top
+        frow[pl.ds(64, 64), pl.ds(t * NB, NB)] = low
+    at = lax.broadcasted_iota(jnp.int32, (seqs, NB), 0)
+    lane = lax.broadcasted_iota(jnp.int32, (seqs, NB), 1)
+    seq = 2 * (at - jnp.where(at >= 64, 64, 0)) + jnp.where(at >= 64, 1, 0)
+    wanted = jnp.logical_and(jnp.logical_and(lane >= heads, lane < heads + per), seq == per * r + lane - heads)
+    pick = jnp.where(wanted, jnp.float32(seqs), 0.0)
+    keep(*split3(jnp.where(lane < 32, pick, frow[:, :NB])), pl.ds(n, NB))
+    keep(*split3(frow[:, NB:]), pl.ds(n + NB, NB))
+    upd[...] = tdot(frow[...], fcol[...], HI) * (1.0 / seqs)
+
+    for b in range(nb):
+        rows = pl.ds(b * NB, NB)
+        u[rows, pl.ds(pl.multiple_of(k * HALF, HALF), HALF)] = x[rows, :HALF]
+        u[rows, pl.ds(pl.multiple_of((1 - k) * HALF, HALF), HALF)] = y[rows, :]
+        u[rows, n:n + NB] = jnp.where(lane < heads, x[rows, HALF:], jnp.where(lane < 32, 0.0, gp[rows, :NB]))
+        u[rows, n + NB:] = gp[rows, NB:]
+        cs = pl.ds(b * NB, width - b * NB)
+        u[rows, cs] = u[rows, cs] + product(rows, cs) * (1.0 / seqs)
+
     row = lax.broadcasted_iota(jnp.int32, (8, NB), 0)
     col = lax.broadcasted_iota(jnp.int32, (8, NB), 1)
-    tdot = lambda a, b: lax.dot_general(a, b, (((0,), (0,)), ((), ())), precision=HI, preferred_element_type=jnp.float32)
-
-    for b in range(nb):
-        rows = pl.ds(b * NB, NB)
-        u_ref[rows, pl.ds(pl.multiple_of(k * HALF, HALF), HALF)] = x[rows, :HALF]
-        u_ref[rows, pl.ds(pl.multiple_of((1 - k) * HALF, HALF), HALF)] = y[rows, :]
-        lhs = f0[:, b * NB:(b + 1) * NB]
-        u_ref[rows, :n] = u_ref[rows, :n] + tdot(lhs, f0[...]) * (1.0 / seqs)
-        low = lane[:NB, :NB]
-        base = jnp.where(low < heads, x[rows, HALF:], jnp.where(low < 32, 0.0, gp[rows, :NB]))
-        extra = tdot(lhs, z)
-        u_ref[rows, n:n + NB] = base + extra[:, :NB]
-        u_ref[rows, n + NB:] = gp[rows, NB:] + extra[:, NB:]
 
     def outer(b, _):
         o = pl.multiple_of(b * NB, NB)
-        A = [u_ref[pl.ds(o + 8 * p, 8), pl.ds(o, NB)] for p in range(16)]
-        V = [jnp.where(col == row + 8 * p, 1.0, 0.0) for p in range(16)]
+        rows = pl.ds(o, NB)
+        A = [u[pl.ds(o + 8 * p, 8), rows] for p in range(NB // 8)]
+        V = [jnp.where(col == row + 8 * p, 1.0, 0.0) for p in range(NB // 8)]
         A, V = factor_block(A, V)
-        for p in range(16):
-            inv_ref[pl.ds(8 * p, 8), :] = V[p]
-        u_ref[pl.ds(o, NB), :] = jnp.dot(inv_ref[...], u_ref[pl.ds(o, NB), :], precision=HI, preferred_element_type=jnp.float32)
-        for p in range(16):
-            u_ref[pl.ds(o + 8 * p, 8), pl.ds(o, NB)] = jnp.where(col >= row + 8 * p, A[p], 0.0)
-
-        def trail(q, _):
-            oq = pl.multiple_of(q * NB, NB)
-            lhs = u_ref[pl.ds(o, NB), pl.ds(oq, NB)]
-            u_ref[pl.ds(oq, NB), :] = u_ref[pl.ds(oq, NB), :] - tdot(lhs, u_ref[pl.ds(o, NB), :])
-            return 0
-        lax.fori_loop(b + 1, nb, trail, 0)
+        for p in range(NB // 8):
+            inv[pl.ds(8 * p, 8), :] = V[p]
+        ih, im, il = split3(inv[...])
+        hh_l, ml_l, mh_l = (jnp.concatenate(pair, 1) for pair in ((ih, ih), (im, il), (im, ih)))
+
+        def dot(a, top, low):
+            return jnp.dot(a, jnp.concatenate([top, low], 0), preferred_element_type=jnp.float32)
+
+        def scale(lo, hi):
+            for t in range(lo, hi, 256):
+                cs = pl.ds(t, 256)
+                h, m, l = split3(u[rows, cs])
+                new = dot(hh_l, h, m) + (dot(ml_l, h, h) + dot(mh_l, m, l))
+                u[rows, cs] = new
+                keep(*split3(new), cs)
+
+        @pl.when(b < nb // 2)
+        def _():
+            scale(0, half)
+        scale(half, width)
+        for p in range(NB // 8):
+            u[pl.ds(o + 8 * p, 8), rows] = jnp.where(col >= row + 8 * p, A[p], 0.0)
+
+        def trail(lo):
+            def body(q, _):
+                qs = pl.ds(pl.multiple_of(q * NB, NB), NB)
+                cs = pl.ds(lo, width - lo)
+                u[qs, cs] = u[qs, cs] - product(qs, cs)
+                return 0
+            return body
+        lax.fori_loop(b + 1, nb // 2, trail(0), 0)
+        lax.fori_loop(jnp.maximum(b + 1, nb // 2), nb, trail(half), 0)
         return 0
     lax.fori_loop(0, nb, outer, 0)
 
-
-def factored(x, y, gp, f0, frow):
-    n = x.shape[0]
+    extra = pl.ds(n, width - n)
+    both[...] = tdot(u[:, n:n + NB], u[:, n:], HI)[:heads]
+    own[...] = u[pl.ds(pl.multiple_of(32 * r, 32), 32), n:n + NB]
+    mine = pl.ds(pl.multiple_of(64 * c, 64), 64)
+    tile = pltpu.roll(u[mine, pl.ds(pl.multiple_of((r // 4) * NB, NB), NB)], lax.rem(128 - 32 * lax.rem(r, 4), 128), 1)
+    down = lax.broadcasted_iota(jnp.int32, (64, NB), 0) + 64 * c
+    tile = jnp.where(lane64 + 32 * r >= down, tile, 0.0)
+    strip[:, :NB] = jnp.where(lane64 < 32, tile, u[mine, n:n + NB])
+    strip[:, NB:] = u[mine, n + NB:]
+
+
+def factored(x, y, gp, all3, col_all):
+    n, f32 = x.shape[0], jnp.float32
     vm = pl.BlockSpec(memory_space=pltpu.VMEM)
+    packed = pltpu.VMEM((2 * NB, n + 256), jnp.bfloat16)
     return pl.pallas_call(
         factor_kernel,
-        out_shape=jax.ShapeDtypeStruct((n, n + 256), jnp.float32),
-        in_specs=[vm] * 5, out_specs=vm,
-        scratch_shapes=[pltpu.VMEM((NB, NB), jnp.float32)],
-        compiler_params=pltpu.CompilerParams(vmem_limit_bytes=40 << 20),
+        out_shape=(
+            jax.ShapeDtypeStruct((256, 512), f32), jax.ShapeDtypeStruct((16, 256), f32),
+            jax.ShapeDtypeStruct((64, 256), f32), jax.ShapeDtypeStruct((32, 128), f32)),
+        in_specs=[vm] * 5, out_specs=(vm,) * 4,
+        scratch_shapes=[
+            pltpu.VMEM((n, n + 256), f32), pltpu.VMEM((NB, NB), f32), packed, packed, packed, packed,
+            pltpu.VMEM((512, NB), f32), pltpu.VMEM((NB, 256), f32), pltpu.VMEM((NB, 512), f32)],
+        compiler_params=pltpu.CompilerParams(vmem_limit_bytes=20 << 20),
         name="factor",
-    )(x, y, gp, f0, frow)
+    )(x, y, gp, all3, col_all)
+
+
+def features_kernel(tok, cot, wts, proj_in, proj_out, live, fp, block):
+    f32 = jnp.float32
+    hidden = 448
+    depth, step = tok.shape[1], 512
+
+    def body(i, acc):
+        at = pl.multiple_of(i * step, step)
+        cs, t = pl.ds(at, step), tok[:, pl.ds(at, step)]
+        g, h, p = acc
+        return (g + jnp.dot(t, wts[cs, :512], preferred_element_type=f32),
+                h + jnp.dot(cot[:, cs], wts[cs, 384:], preferred_element_type=f32),
+                p + jnp.dot(t, proj_in[cs, :], preferred_element_type=f32))
+    rows = tok.shape[0]
+    g, h, p = lax.fori_loop(0, depth // step, body, (
+        jnp.zeros((rows, 512), f32), jnp.zeros((rows, 512), f32), jnp.zeros((rows, 128), f32)))
+    h = pltpu.roll(h, 512 - 64, 1)
+    lane = lax.broadcasted_iota(jnp.int32, (rows, 512), 1)
+    up = jnp.where(lane < hidden, h * (g / (1.0 + jnp.exp(-g))), 0.0).astype(jnp.bfloat16)
+    outer = jnp.dot(up, proj_out[...], preferred_element_type=f32)
+    p = p * live[...]
+    for s in range(2):
+        total = jnp.zeros((128, 128), f32)
+        for e in range(2):
+            ts = slice((2 * s + e) * 64, (2 * s + e + 1) * 64)
+            o = outer[ts] if e == 0 else pltpu.roll(outer[ts], 64, 1)
+            total = total + tdot(p[ts], o, HI)
+        block[...] = total
+        for c in range(16):
+            fp[c, pl.ds(8 * s, 8), :] = block[pl.ds(c, 8, stride=16), :]
 
 
 def local(tokens, cotangent, gate_weight, down_weight, proj_in, proj_out, lengths, loss_mask, gram_in, queries):
@@ -513,62 +630,42 @@
     k = lax.rem(c, NC)
     cycles, band_rows, _, band_cols = gram_in.shape
     seq_count, window = loss_mask.shape
-    hidden = gate_weight.shape[1]
-    rows, cols = NZ * NX, NY * NC
-    seqs = seq_count * rows
-    pw = band_rows * rows
+    vm = pl.BlockSpec(memory_space=pltpu.VMEM)
 
     weights = jnp.concatenate([gate_weight, down_weight], axis=1)
     band = gram_in[:, :, 0, :].reshape(cycles * band_rows, band_cols).T
+    positions = jnp.arange(window, dtype=jnp.int32)
+    live = (positions[None, :] >= (window - lengths)[:, None]).astype(f32) * loss_mask.astype(f32)
+    outer_in = jnp.pad(proj_out, ((0, 512 - proj_out.shape[0]), (0, 128 - proj_out.shape[1])))
+    live = jnp.broadcast_to(live.reshape(seq_count * window, 1), (seq_count * window, proj_in.shape[1]))
+    weights, band, outer_in, live = lax.optimization_barrier((weights, band, outer_in, live))
     tok, cot, wts, gp = gather(tokens, cotangent, weights, band)
 
+    fp = pl.pallas_call(
+        features_kernel,
+        out_shape=jax.ShapeDtypeStruct((NY * NC, 16, 128), f32),
+        in_specs=[vm] * 6, out_specs=vm,
+        scratch_shapes=[pltpu.VMEM((128, 128), f32)],
+        compiler_params=pltpu.CompilerParams(vmem_limit_bytes=12 << 20),
+        name="features",
+    )(tok, cot, wts, proj_in, outer_in, live)
+
+    gp, fp = lax.optimization_barrier((gp, fp))
     diag = gp[:, :band_rows].T
     diag = lax.dynamic_slice_in_dim(diag, k * HALF, HALF, 1)
     head = jnp.pad(queries[:, 0, :].T, ((0, 0), (0, 128 - queries.shape[0])))
     dp = jnp.concatenate([diag, head], axis=1)
 
-    gate_pre = jnp.dot(tok, wts[:, :512], preferred_element_type=f32)[:, :hidden]
-    grad_hidden = jnp.dot(cot, wts[:, 384:], preferred_element_type=f32)[:, hidden - 384:]
-    grad_up = (grad_hidden * jax.nn.silu(gate_pre)).astype(jnp.bfloat16)
-    outer = jnp.dot(grad_up, proj_out, preferred_element_type=f32)
-    inner = jnp.dot(tok, proj_in, preferred_element_type=f32)
-    positions = jnp.arange(window, dtype=jnp.int32)
-    live = (positions[None, :] >= (window - lengths)[:, None]).astype(f32) * loss_mask.astype(f32)
-    weighted = inner.reshape(seq_count, window, -1) * live[:, :, None]
-    feats = jnp.einsum("stk,stl->skl", weighted, outer.reshape(seq_count, window, -1), precision=HI)
-    width = feats.shape[2]
-    fp = feats.reshape(seq_count, cycles, cols, width).transpose(2, 1, 0, 3).reshape(cols, 16, 128)
-
     col_all, all3, d_own, d_other = exchange(fp, dp)
-
-    fcol = col_all.reshape(rows, cycles, seq_count, width).transpose(0, 2, 1, 3).reshape(seqs, cycles * width)
-    take = all3.reshape(cols, TAKE, 128)
-    f0 = take[:, :64].reshape(cols, seqs, width).transpose(1, 0, 2).reshape(seqs, cols * width)
-    frow = take[:, 64:].reshape(cols, 2, cycles, seq_count, width)
-    frow = lax.dynamic_slice_in_dim(frow, lax.rem(r, 2) * band_rows, band_rows, 4)
-    frow = frow.transpose(0, 1, 3, 2, 4).reshape(seqs, cycles * band_rows)
-
-    u = factored(d_own, d_other, gp, f0, frow)
-
-    update = lax.dot_general(frow, fcol, (((0,), (0,)), ((), ())), precision=HI, preferred_element_type=f32) / seqs
-    updated = gram_in + update.reshape(cycles, band_rows, cycles, band_cols)
-    strip = lax.dynamic_slice_in_dim(u, c * band_cols, band_cols, 0)
-    tile = lax.dynamic_slice_in_dim(strip, r * band_rows, band_rows, 1)
-    at_row = lax.broadcasted_iota(jnp.int32, tile.shape, 1) + r * band_rows
-    at_col = lax.broadcasted_iota(jnp.int32, tile.shape, 0) + c * band_cols
-    tile = jnp.where(at_row >= at_col, tile, 0.0)
-    strip = jnp.concatenate([tile, strip[:, pw + band_rows:]], axis=1)
+    upd, both, strip, own = factored(d_own, d_other, gp, all3, col_all)
+
     panel = strip.T.reshape(cycles, band_rows, 1, band_cols)
-    gram_next = jnp.concatenate([panel, updated[:, :, 1:]], axis=2)
-
+    which = lax.broadcasted_iota(jnp.int32, gram_in.shape, 2)
+    gram_next = jnp.where(which == 0, panel, gram_in + upd.reshape(gram_in.shape))
     count = queries.shape[0]
-    extra = u[:, pw:]
-    solved = extra[:, :count]
-    both = lax.dot_general(solved, extra, (((0,), (0,)), ((), ())), precision=HI, preferred_element_type=f32)
     scores = both[:, count:count + seq_count]
     tail = queries[:, 1:] - both[:, band_rows:].reshape(count, cycles - 1, band_rows)
-    own = lax.dynamic_slice_in_dim(solved, r * band_rows, band_rows, 0).T
-    query_next = jnp.concatenate([own[:, None], tail], axis=1)
+    query_next = jnp.concatenate([own[:, :count].T[:, None], tail], axis=1)
     return gram_next, query_next, scores
 
 

time: 269 us -> 174 us (0.65)
  Pallas kernels: 210 us -> 162 us
  local copies, waits for them, and re-layouts: 34.9 us -> 7.25 us
  matrix products: 15.1 us -> 0 us
  other arithmetic: 7.1 us -> 3.36 us
    pallas_call x1 -> x2, Pallas kernels: 96.5 us -> 55.5 us  [the longest x1 49.5 us: factored(): pl.pallas_call(factor_kernel, out_shape=(jax.ShapeDtypeStruct((256, 512),...]
    dot_general x6 -> x0, matrix products: 15.1 us -> none  [the longest x1 6.53 us: local(): outer = jnp.dot(grad_up, proj_out, preferred_element_type=f32)]
    unnamed x34 -> x15, local copies, waits for them, and re-layouts: 18 us -> 4.72 us
    reshape x10 -> x1, local copies, waits for them, and re-layouts: 9 us -> 0.2 us  [local(): upd.reshape(gram_in.shape)]
    pallas_call x1, Pallas kernels: 51.4 us -> 45 us  [exchange(): pl.pallas_call(body, out_shape=(jax.ShapeDtypeStruct((rows * 16, 128), f3...]
    transpose x4 -> x0, local copies, waits for them, and re-layouts: 3.92 us -> none  [the longest x2 2.22 us: local(): frow = frow.transpose(0, 1, 3, 2, 4).reshape(seqs, cycles * band_rows)]
    add x3 -> x0, other arithmetic: 2.72 us -> none  [the longest x1 2.72 us: local(): updated = gram_in + update.reshape(cycles, band_rows, cycles, band_cols)]
where the time goes in v2:
time: 174 us
  Pallas kernels  162 us (93%)
  local copies, waits for them, and re-layouts  7.25 us (4%)
  other arithmetic  3.36 us (2%)
    pallas_call x1, Pallas kernels, gather(): pl.pallas_call(body, out_shape=(jax.ShapeDtypeStruct((tok.shape[0], tok.s...  61.8 us
    pallas_call x1, Pallas kernels, factored(): pl.pallas_call(factor_kernel, out_shape=(jax.ShapeDtypeStruct((256, 512),...  49.5 us
    pallas_call x1, Pallas kernels, exchange(): pl.pallas_call(body, out_shape=(jax.ShapeDtypeStruct((rows * 16, 128), f3...  45 us
    pallas_call x1, Pallas kernels, local(): pl.pallas_call(features_kernel, out_shape=jax.ShapeDtypeStruct((NY * NC,...  5.96 us
    unnamed x15, local copies, waits for them, and re-layouts  4.72 us

profile of v2, /device:TPU:1, one launch (start us, length us, event | category | flops | bytes accessed | tf_op | source)
XLA Modules:
  0.0 173.7 jit_solution(16353409089936684989)
XLA Ops:
  0.6 0.0 copy-start.1
  0.6 0.0 copy-start.2
  0.7 0.0 copy-start
  0.7 1.1 copy.23
  1.8 1.0 copy.22
  2.8 0.1 pad_maximum_fusion.refs_2_
  2.9 1.3 slice.21
  4.2 0.1 copy.24
  4.3 1.0 copy.25
  5.3 0.7 broadcast_subtract_fusion
  6.0 0.8 convert_select_fusion
  6.7 0.1 broadcast_in_dim.22
  6.8 0.1 broadcast_in_dim.23.live
  6.9 0.0 copy-done.1
  6.9 0.0 copy-done.2
  6.9 61.8 %gather.1 = (bf16[256,4096]{1,0:T(8,128)(2,1)S(1)}, bf16[256,4096]{1,0:T(8,128)(2,1)S(1)}, bf16[4096,896]{1,0:T(8,128)(2,1)S(1)}, f32[1024,256]{1,0:T(8,128)S(1)}) custom-call(bf16[256,256]{1,0:T(8,128)(2,1)S(1)} %copy-done.1, bf16[256,256]{1,0:T(8,128)(2,1)S(1)} %copy-done.2, bf16[128,896]{1,0:T(8,128)(2,1)S(1)} %pad_maximum_fusion.refs_2_, ...), custom_call_target="tpu_custom_call" | custom-call | tf_op jit(solution)/shard_map/gather/pallas_call | solution.py:179
  68.7 0.0 copy-done
  68.7 0.0 slice-start
  68.7 6.0 %features.1.refs_0_ = f32[16,16,128]{2,1,0:T(8,128)S(1)} custom-call(bf16[256,4096]{1,0:T(8,128)(2,1)S(1)} %get-tuple-element.24.tok, bf16[256,4096]{1,0:T(8,128)(2,1)S(1)} %get-tuple-element.25.cot, bf16[4096,896]{1,0:T(8,128)(2,1)S(1)} %get-tuple-element.26.wts, bf16[4096,128]{1,0:T(8,128)(2,1)S(1)} %copy-done, bf16[512,128]{1,0:T(8,128)(2,1)S(1)} %pad.8.proj_out, ...), custom_call_target="tpu_custom_call" | custom-call | tf_op jit(solution)/shard_map/features/pallas_call | solution.py:644
  74.7 0.0 slice-done
  74.7 0.1 copy.31
  74.8 0.3 copy.26
  75.2 45.0 %exchange.1 = (f32[512,128]{1,0:T(8,128)S(1)}, f32[1536,128]{1,0:T(8,128)S(1)}, f32[1024,640]{1,0:T(8,128)S(1)}, f32[1024,512]{1,0:T(8,128)S(1)}) custom-call(f32[16,16,128]{2,1,0:T(8,128)S(1)} %features.1.refs_0_, f32[32,640]{1,0:T(8,128)S(1)} %select_maximum_fusion.refs_1_), custom_call_target="tpu_custom_call" | custom-call | tf_op jit(solution)/shard_map/exchange/pallas_call | solution.py:372
  120.2 49.5 %factor.1 = (f32[256,512]{1,0:T(8,128)S(1)}, f32[16,256]{1,0:T(8,128)S(1)}, f32[64,256]{1,0:T(8,128)S(1)}, f32[32,128]{1,0:T(8,128)S(1)}) custom-call(f32[1024,640]{1,0:T(8,128)S(1)} %get-tuple-element.31.x, f32[1024,512]{1,0:T(8,128)S(1)} %get-tuple-element.32.y, f32[1024,256]{1,0:T(8,128)S(1)} %get-tuple-element.30.gp, ...), custom_call_target="tpu_custom_call" | custom-call | tf_op jit(solution)/shard_map/factor/pallas_call | solution.py:582
  169.7 0.0 copy-start.3
  169.7 0.2 reshape.17
  169.9 0.0 copy-start.4
  169.9 0.1 copy.28
  170.0 0.9 copy-done.3
  170.9 1.2 add_select_fusion
  172.1 0.1 slice.26
  172.2 0.1 reshape.18
  172.3 0.0 copy-done.4
  172.3 0.1 copy.29
  172.4 0.7 pad_maximum_fusion.1
  173.0 0.1 slice.27
  173.1 0.7 copy.30
  (7 shorter events, 0.1 us)
Async XLA Ops:
  0.6 6.3 %copy-start.1 = (bf16[256,256]{1,0:T(8,128)(2,1)S(1)}, bf16[256,256]{1,0:T(8,128)(2,1)}, u32[]{:S(2)}) copy-start(bf16[256,256]{1,0:T(8,128)(2,1)} %refs_0_.1) | copy-start | bytes 393220
  0.6 6.3 %copy-start.2 = (bf16[256,256]{1,0:T(8,128)(2,1)S(1)}, bf16[256,256]{1,0:T(8,128)(2,1)}, u32[]{:S(2)}) copy-start(bf16[256,256]{1,0:T(8,128)(2,1)} %refs_1_.1) | copy-start | bytes 393220
  0.7 68.0 %copy-start = (bf16[4096,128]{1,0:T(8,128)(2,1)S(1)}, bf16[4096,128]{1,0:T(8,128)(2,1)}, u32[]{:S(2)}) copy-start(bf16[4096,128]{1,0:T(8,128)(2,1)} %proj_in.1) | copy-start | bytes 3145732
  68.7 6.0 %slice-start = ((f32[16,8,32]{2,1,0:T(8,128)}), f32[16,1,32]{2,1,0:T(1,128)S(1)}, s32[]{:S(2)}) async-start(f32[16,8,32]{2,1,0:T(8,128)} %param.19), calls=%async_computation | async-start | bytes 16384 | tf_op jit(solution)/shard_map/slice | solution.py:656
  169.7 1.2 copy-start.3
  169.9 2.3 %copy-start.4 = (f32[16,8,32]{2,1,0:T(8,128)S(1)}, f32[16,8,32]{2,1,0:T(8,128)}, u32[]{:S(2)}) copy-start(f32[16,8,32]{2,1,0:T(8,128)} %param.19) | copy-start | bytes 49156

commit v3 on v2

--- a/solution.py
+++ b/solution.py
@@ -210,15 +210,15 @@
 
 HALF = 512
 TAKE = 96
-SUM_AT, SPREAD_AT, PANEL_AT = 6.0, 10.0, 19.0
-
-
-def exchange_kernel(msgs, times, fp, dp, col_all, all3, d_all, d_other,
-                    parts, hbuf, p3, dsend, drecv, s1, r1, s2, r2, sl, rl, s3, r3, s4, r4, own):
+BEGIN_AT, SUM_AT, SPREAD_AT, PANEL_AT = 3.2, 9.0, 13.0, 21.0
+
+
+def exchange_kernel(msgs, times, tok, cot, wts, proj_in, proj_out, live, gp, head, col_all, all3, d_all, d_other,
+                    fp, dp, block, parts, hbuf, p3, dsend, drecv, s1, r1, s2, r2, sl, rl, s3, r3, s4, r4, own):
     me = position()
     r, c = lax.axis_index("rows"), lax.axis_index("cols")
     here, core = (0, 0, 0, 0), (0, 0, 0, 1)
-    band = dp.shape[0]
+    band = head.shape[0]
     half = band // 2
 
     def rdma(src, dst, send, recv, to):
@@ -259,7 +259,6 @@
         return y * NC + k
 
     kept = pltpu.make_async_copy(dp, d_all.at[pl.ds(pl.multiple_of(r * band, 8), band), :], own)
-    kept.start()
     both = sorted(set(cols_off + rows_off))
     barrier = pltpu.get_barrier_semaphore()
     for o in both:
@@ -268,8 +267,6 @@
         @pl.when(jnp.logical_not(at_home[e]))
         def _():
             pl.semaphore_signal(barrier, inc=1, device_id=legs[e], device_id_type=MESH)
-    pl.semaphore_wait(barrier, jnp.where(c == r // 2, len(both) + 1, len(both) + 2))
-
     first = [rdma(fp.at[col_of(o)], parts.at[i], s1.at[i], r1.at[i], device(me, o)) for i, o in enumerate(cols_off)]
     my_rows = pl.ds(pl.multiple_of(r * 16, 16), 16)
     second = [rdma(hbuf, col_all.at[my_rows, :], s2.at[i], r2.at[i], device(me, o)) for i, o in enumerate(rows_off)]
@@ -327,16 +324,27 @@
             rdma(there, there, s3.at[i], r3.at[i], device(me, o)).wait_recv()
             give(i + 1).start()
 
-    for copy in first:
-        copy.start()
+    mine = gp[pl.ds(pl.multiple_of(lax.rem(c, NC) * HALF, HALF), HALF), :128]
+    dp[:, :HALF] = mine.T[:band]
+    dp[:, HALF:] = head[...]
+    sums = features_part(tok, cot, wts, proj_in, 0, 5, None)
+    pl.semaphore_wait(barrier, jnp.where(c == r // 2, len(both) + 1, len(both) + 2))
+    kept.start()
     for n, m in enumerate(msgs):
         if m.dep is None:
             dcopy(n).start()
+    sums = features_part(tok, cot, wts, proj_in, 5, 8, sums)
+    features_end(sums, proj_out, live, fp, block)
+
+    def begin():
+        for copy in first:
+            copy.start()
+
     events = sorted([(times[n], n) for n in range(len(msgs))]
-                    + [(SUM_AT, -1), (SPREAD_AT, -2), (PANEL_AT, -3)])
+                    + [(BEGIN_AT, -4), (SUM_AT, -1), (SPREAD_AT, -2), (PANEL_AT, -3)])
     for _, n in events:
         if n < 0:
-            (sum_up, spread, panel)[-n - 1]()
+            (sum_up, spread, panel, begin)[-n - 1]()
             continue
         darrived(n)
         for f, m in enumerate(msgs):
@@ -359,8 +367,45 @@
     kept.wait()
 
 
-def exchange(fp, dp):
-    msgs = exchange_messages(dp.size * 2)
+def features_part(tok, cot, wts, proj_in, lo, hi, sums):
+    f32 = jnp.float32
+    rows, step = tok.shape[0], 512
+
+    def body(i, acc):
+        cs = pl.ds(pl.multiple_of(i * step, step), step)
+        t = tok[:, cs]
+        g, h, p = acc
+        return (g + jnp.dot(t, wts[cs, :512], preferred_element_type=f32),
+                h + jnp.dot(cot[:, cs], wts[cs, 384:], preferred_element_type=f32),
+                p + jnp.dot(t, proj_in[cs, :], preferred_element_type=f32))
+    if sums is None:
+        sums = (jnp.zeros((rows, 512), f32), jnp.zeros((rows, 512), f32), jnp.zeros((rows, 128), f32))
+    return lax.fori_loop(lo, hi, body, sums)
+
+
+def features_end(sums, proj_out, live, fp, block):
+    f32 = jnp.float32
+    hidden = 448
+    g, h, p = sums
+    h = pltpu.roll(h, 512 - 64, 1)
+    lane = lax.broadcasted_iota(jnp.int32, h.shape, 1)
+    up = jnp.where(lane < hidden, h * (g / (1.0 + jnp.exp(-g))), 0.0).astype(jnp.bfloat16)
+    outer = jnp.dot(up, proj_out[...], preferred_element_type=f32)
+    p = p * live[...]
+    for s in range(2):
+        total = jnp.zeros((128, 128), f32)
+        for e in range(2):
+            ts = slice((2 * s + e) * 64, (2 * s + e + 1) * 64)
+            o = outer[ts] if e == 0 else pltpu.roll(outer[ts], 64, 1)
+            total = total + tdot(p[ts], o, HI)
+        block[...] = total
+        for c in range(16):
+            fp[c, pl.ds(8 * s, 8), :] = block[pl.ds(c, 8, stride=16), :]
+
+
+def exchange(tok, cot, wts, proj_in, proj_out, live, gp, head):
+    band, wide = head.shape[0], HALF + head.shape[1]
+    msgs = exchange_messages(band * wide * 2)
     times = ordered(msgs)
     vm = pl.BlockSpec(memory_space=pltpu.VMEM)
     f32 = jnp.float32
@@ -374,16 +419,17 @@
         out_shape=(
             jax.ShapeDtypeStruct((rows * 16, 128), f32),
             jax.ShapeDtypeStruct((cols * TAKE, 128), f32),
-            jax.ShapeDtypeStruct((rows * dp.shape[0], dp.shape[1]), f32),
-            jax.ShapeDtypeStruct((rows * dp.shape[0], HALF), f32)),
-        in_specs=[vm] * 2, out_specs=(vm,) * 4,
+            jax.ShapeDtypeStruct((rows * band, wide), f32),
+            jax.ShapeDtypeStruct((rows * band, HALF), f32)),
+        in_specs=[vm] * 8, out_specs=(vm,) * 4,
         scratch_shapes=[
+            pltpu.VMEM((cols, 16, 128), f32), pltpu.VMEM((band, wide), f32), pltpu.VMEM((128, 128), f32),
             pltpu.VMEM((cols - 1, 16, 128), f32), pltpu.VMEM((16, 128), f32), pltpu.VMEM((TAKE, 128), f32),
             dma((len(msgs),)), dma((len(msgs),)), dma((cols - 1,)), dma((cols - 1,)), dma((rows - 1,)), dma((rows - 1,)),
             dma((2,)), dma((2,)), dma((NY - 1,)), dma((NY - 1,)), dma((NY,)), dma((NY,)), dma],
-        compiler_params=pltpu.CompilerParams(collective_id=1, has_side_effects=True, vmem_limit_bytes=4 << 20),
+        compiler_params=pltpu.CompilerParams(collective_id=1, has_side_effects=True, vmem_limit_bytes=14 << 20),
         name="exchange",
-    )(fp, dp)
+    )(tok, cot, wts, proj_in, proj_out, live, gp, head)
 
 
 def lanes(x, j):
@@ -593,44 +639,10 @@
     )(x, y, gp, all3, col_all)
 
 
-def features_kernel(tok, cot, wts, proj_in, proj_out, live, fp, block):
-    f32 = jnp.float32
-    hidden = 448
-    depth, step = tok.shape[1], 512
-
-    def body(i, acc):
-        at = pl.multiple_of(i * step, step)
-        cs, t = pl.ds(at, step), tok[:, pl.ds(at, step)]
-        g, h, p = acc
-        return (g + jnp.dot(t, wts[cs, :512], preferred_element_type=f32),
-                h + jnp.dot(cot[:, cs], wts[cs, 384:], preferred_element_type=f32),
-                p + jnp.dot(t, proj_in[cs, :], preferred_element_type=f32))
-    rows = tok.shape[0]
-    g, h, p = lax.fori_loop(0, depth // step, body, (
-        jnp.zeros((rows, 512), f32), jnp.zeros((rows, 512), f32), jnp.zeros((rows, 128), f32)))
-    h = pltpu.roll(h, 512 - 64, 1)
-    lane = lax.broadcasted_iota(jnp.int32, (rows, 512), 1)
-    up = jnp.where(lane < hidden, h * (g / (1.0 + jnp.exp(-g))), 0.0).astype(jnp.bfloat16)
-    outer = jnp.dot(up, proj_out[...], preferred_element_type=f32)
-    p = p * live[...]
-    for s in range(2):
-        total = jnp.zeros((128, 128), f32)
-        for e in range(2):
-            ts = slice((2 * s + e) * 64, (2 * s + e + 1) * 64)
-            o = outer[ts] if e == 0 else pltpu.roll(outer[ts], 64, 1)
-            total = total + tdot(p[ts], o, HI)
-        block[...] = total
-        for c in range(16):
-            fp[c, pl.ds(8 * s, 8), :] = block[pl.ds(c, 8, stride=16), :]
-
-
 def local(tokens, cotangent, gate_weight, down_weight, proj_in, proj_out, lengths, loss_mask, gram_in, queries):
     f32 = jnp.float32
-    r, c = lax.axis_index("rows"), lax.axis_index("cols")
-    k = lax.rem(c, NC)
     cycles, band_rows, _, band_cols = gram_in.shape
     seq_count, window = loss_mask.shape
-    vm = pl.BlockSpec(memory_space=pltpu.VMEM)
 
     weights = jnp.concatenate([gate_weight, down_weight], axis=1)
     band = gram_in[:, :, 0, :].reshape(cycles * band_rows, band_cols).T
@@ -638,25 +650,11 @@
     live = (positions[None, :] >= (window - lengths)[:, None]).astype(f32) * loss_mask.astype(f32)
     outer_in = jnp.pad(proj_out, ((0, 512 - proj_out.shape[0]), (0, 128 - proj_out.shape[1])))
     live = jnp.broadcast_to(live.reshape(seq_count * window, 1), (seq_count * window, proj_in.shape[1]))
-    weights, band, outer_in, live = lax.optimization_barrier((weights, band, outer_in, live))
+    head = jnp.pad(queries[:, 0, :].T, ((0, 0), (0, 128 - queries.shape[0])))
+    weights, band, outer_in, live, head = lax.optimization_barrier((weights, band, outer_in, live, head))
     tok, cot, wts, gp = gather(tokens, cotangent, weights, band)
 
-    fp = pl.pallas_call(
-        features_kernel,
-        out_shape=jax.ShapeDtypeStruct((NY * NC, 16, 128), f32),
-        in_specs=[vm] * 6, out_specs=vm,
-        scratch_shapes=[pltpu.VMEM((128, 128), f32)],
-        compiler_params=pltpu.CompilerParams(vmem_limit_bytes=12 << 20),
-        name="features",
-    )(tok, cot, wts, proj_in, outer_in, live)
-
-    gp, fp = lax.optimization_barrier((gp, fp))
-    diag = gp[:, :band_rows].T
-    diag = lax.dynamic_slice_in_dim(diag, k * HALF, HALF, 1)
-    head = jnp.pad(queries[:, 0, :].T, ((0, 0), (0, 128 - queries.shape[0])))
-    dp = jnp.concatenate([diag, head], axis=1)
-
-    col_all, all3, d_own, d_other = exchange(fp, dp)
+    col_all, all3, d_own, d_other = exchange(tok, cot, wts, proj_in, outer_in, live, gp, head)
     upd, both, strip, own = factored(d_own, d_other, gp, all3, col_all)
 
     panel = strip.T.reshape(cycles, band_rows, 1, band_cols)

time: 174 us -> 172 us (0.989)
  Pallas kernels: 162 us -> 160 us
    pallas_call x1 -> x0, Pallas kernels: 5.96 us -> none  [local(): pl.pallas_call(features_kernel, out_shape=jax.ShapeDtypeStruct((NY * NC,...]
    pallas_call x1, Pallas kernels: 45 us -> 48.9 us  [exchange(): pl.pallas_call(body, out_shape=(jax.ShapeDtypeStruct((rows * 16, 128), f3...]
where the time goes in v3:
time: 172 us; the launch traced here: 171 us
  Pallas kernels  160 us (93%)
  local copies, waits for them, and re-layouts  6.86 us (4%)
  other arithmetic  3.36 us (2%)
    pallas_call x1, Pallas kernels, gather(): pl.pallas_call(body, out_shape=(jax.ShapeDtypeStruct((tok.shape[0], tok.s...  61.8 us
    pallas_call x1, Pallas kernels, factored(): pl.pallas_call(factor_kernel, out_shape=(jax.ShapeDtypeStruct((256, 512),...  49.5 us
    pallas_call x1, Pallas kernels, exchange(): pl.pallas_call(body, out_shape=(jax.ShapeDtypeStruct((rows * 16, 128), f3...  48.9 us
    unnamed x15, local copies, waits for them, and re-layouts  3.84 us

profile of v3, /device:TPU:1, one launch (start us, length us, event | category | flops | bytes accessed | tf_op | source)
XLA Modules:
  0.0 171.2 jit_solution(1154618155347706691)
XLA Ops:
  0.6 0.0 copy-start.1
  0.6 0.0 copy-start.2
  0.7 0.0 copy-start
  0.7 1.1 copy.21
  1.8 1.0 copy.22
  2.8 0.1 pad_maximum_fusion.refs_2_
  2.9 1.0 copy.24
  3.9 1.3 slice.18
  5.2 0.1 copy.23
  5.3 0.7 broadcast_subtract_fusion
  6.0 0.8 convert_select_fusion
  6.7 0.1 broadcast_in_dim.22
  6.8 0.1 broadcast_in_dim.23.refs_5_
  6.9 0.9 slice.19
  7.7 0.1 copy.29
  7.8 0.0 copy-done.1
  7.8 0.0 copy-done.2
  7.8 61.8 %gather.1 = (bf16[256,4096]{1,0:T(8,128)(2,1)S(1)}, bf16[256,4096]{1,0:T(8,128)(2,1)S(1)}, bf16[4096,896]{1,0:T(8,128)(2,1)S(1)}, f32[1024,256]{1,0:T(8,128)S(1)}) custom-call(bf16[256,256]{1,0:T(8,128)(2,1)S(1)} %copy-done.1, bf16[256,256]{1,0:T(8,128)(2,1)S(1)} %copy-done.2, bf16[128,896]{1,0:T(8,128)(2,1)S(1)} %pad_maximum_fusion.refs_2_, ...), custom_call_target="tpu_custom_call" | custom-call | tf_op jit(solution)/shard_map/gather/pallas_call | solution.py:179
  69.6 0.0 copy-done
  69.6 48.9 %exchange.1 = (f32[512,128]{1,0:T(8,128)S(1)}, f32[1536,128]{1,0:T(8,128)S(1)}, f32[1024,640]{1,0:T(8,128)S(1)}, f32[1024,512]{1,0:T(8,128)S(1)}) custom-call(bf16[256,4096]{1,0:T(8,128)(2,1)S(1)} %get-tuple-element.22.refs_0_, bf16[256,4096]{1,0:T(8,128)(2,1)S(1)} %get-tuple-element.23.refs_1_, bf16[4096,896]{1,0:T(8,128)(2,1)S(1)} %get-tuple-element.24.refs_2_, ...), custom_call_target="tpu_custom_call" | custom-call | tf_op jit(solution)/shard_map/exchange/pallas_call | solution.py:417
  118.5 0.0 copy-start.4
  118.5 49.5 %factor.1 = (f32[256,512]{1,0:T(8,128)S(1)}, f32[16,256]{1,0:T(8,128)S(1)}, f32[64,256]{1,0:T(8,128)S(1)}, f32[32,128]{1,0:T(8,128)S(1)}) custom-call(f32[1024,640]{1,0:T(8,128)S(1)} %get-tuple-element.29.x, f32[1024,512]{1,0:T(8,128)S(1)} %get-tuple-element.30.y, f32[1024,256]{1,0:T(8,128)S(1)} %get-tuple-element.27.refs_6_.gp, ...), custom_call_target="tpu_custom_call" | custom-call | tf_op jit(solution)/shard_map/factor/pallas_call | solution.py:628
  168.1 0.0 copy-start.3
  168.1 0.1 slice.22
  168.2 0.1 reshape.18
  168.2 0.0 copy-done.4
  168.3 0.1 copy.27
  168.4 0.7 pad_maximum_fusion.1
  169.0 0.2 reshape.17
  169.2 0.1 copy.26
  169.3 0.0 copy-done.3
  169.3 1.2 add_select_fusion
  170.5 0.1 slice.23
  170.6 0.7 copy.28
  (5 shorter events, 0.1 us)
Async XLA Ops:
  0.6 7.2 %copy-start.1 = (bf16[256,256]{1,0:T(8,128)(2,1)S(1)}, bf16[256,256]{1,0:T(8,128)(2,1)}, u32[]{:S(2)}) copy-start(bf16[256,256]{1,0:T(8,128)(2,1)} %refs_0_.1) | copy-start | bytes 393220
  0.6 7.2 %copy-start.2 = (bf16[256,256]{1,0:T(8,128)(2,1)S(1)}, bf16[256,256]{1,0:T(8,128)(2,1)}, u32[]{:S(2)}) copy-start(bf16[256,256]{1,0:T(8,128)(2,1)} %refs_1_.1) | copy-start | bytes 393220
  0.7 69.0 %copy-start = (bf16[4096,128]{1,0:T(8,128)(2,1)S(1)}, bf16[4096,128]{1,0:T(8,128)(2,1)}, u32[]{:S(2)}) copy-start(bf16[4096,128]{1,0:T(8,128)(2,1)} %refs_3_.1) | copy-start | bytes 3145732
  118.5 49.7 %copy-start.4 = (f32[16,8,32]{2,1,0:T(8,128)S(1)}, f32[16,8,32]{2,1,0:T(8,128)}, u32[]{:S(2)}) copy-start(f32[16,8,32]{2,1,0:T(8,128)} %param.19) | copy-start | bytes 49156
  168.1 1.2 copy-start.3
